TPU v7x, 256 devices: a whole 4x4x8 slice. The times are simulated.
256 devices in a mesh: grp: 128 (over x, y, z), cores: 2 (over core).
Axes of the slice: x: 4, y: 4, z: 8, core: 2. Of those that a mesh axis runs over, the one named last changes fastest.
Arguments:
- invariant_fluid_quantities: float32 [8, 16384, 512], P(None, ('grp', 'cores')), may hold values from -6 to 6
- flux_derivative_matrices: float32 [3, 8, 8], replicated, may hold values from -2 to 2
- levels: int32 [16384], P(('grp', 'cores')), may hold values from 0 to 3
- neighbours: int32 [16384, 6], P(('grp', 'cores')), may hold values from -1 to 16383, as said below
- block_latitude_band: int32 [16384, 1], P(('grp', 'cores')), may hold values from 0 to 127; in each aligned block of 64 rows (0 to 63, 64 to 127, ...) at most 2 rows name the same one
- block_longitude_segment: int32 [16384], P(('grp', 'cores')), may hold values from 0 to 15
- parallel_flow_coefficients: float32 [8], replicated, may hold values from -2 to 2
Outputs:
- state_out: float32 [8, 16384, 512], P(None, ('grp', 'cores'))
- fac_grid: float32 [512, 1024], P(('grp', 'cores'))
- potential: float32 [512, 1024], P(('grp', 'cores'))
- shell_potential: float32 [16384, 128], P(('grp', 'cores'))
Inputs may be any that keep to these rules, and one draw needn't show every extreme that they name: `neighbours`: each entry is -1 or a block held by the same device as the block or by the device just before or after it; device i holds blocks i * 64 to (i + 1) * 64 - 1. `block_latitude_band`: among the 64 blocks of one device no band is named more than 2 times, a bound that some block reaches.
All inputs are finite; a program needn't handle non-finite values.
Results may differ from a plain program's by a relative error of at most 0.0004.
Values sent between devices are 32-bit elements; how exact they have to be, the bound alone decides.
No kernel may reach another device: no remote copies, remote signals or barrier semaphores. Data moves between devices by JAX's collectives and lax.ppermute only.
A program may use at most 128 MiB of HBM per device.

v0:
```python
import math

import jax
import jax.numpy as jnp
from jax import lax
from jax.sharding import PartitionSpec as P

LEVELS = 4
STEPS = 2
LAT_DEV = 2
NLON = 1024
DEGREES = 512


COURANT = 0.3
KAPPA2 = 400.0
POT_GAIN = 2000.0
HIGHEST_PRECISION = lax.Precision.HIGHEST


def passed_along(value, axis, steps):
    count = lax.axis_size(axis)
    leading, last = (max(0, -steps), min(count, count - steps))
    return lax.ppermute(value, axis, [(source, source + steps) for source in range(leading, last)])


def block_faces(state_in):
    state_variables, blocks = (state_in.shape[0], state_in.shape[1])
    block_cube = state_in.reshape(state_variables, blocks, 8, 8, 8)
    layers = [
        block_cube[:, :, 0],
        block_cube[:, :, 7],
        block_cube[:, :, :, 0],
        block_cube[:, :, :, 7],
        block_cube[:, :, :, :, 0],
        block_cube[:, :, :, :, 7],
    ]
    return jnp.stack(
        [one_layer.reshape(state_variables, blocks, 64) for one_layer in layers], axis=2
    )


def spread_face(values, direction):
    state_variables, blocks = (values.shape[0], values.shape[1])
    if direction == 0:
        expanded = jnp.broadcast_to(
            values.reshape(state_variables, blocks, 1, 64), (state_variables, blocks, 8, 64)
        )
    elif direction == 1:
        expanded = jnp.broadcast_to(
            values.reshape(state_variables, blocks, 8, 1, 8), (state_variables, blocks, 8, 8, 8)
        )
    else:
        expanded = jnp.broadcast_to(
            values.reshape(state_variables, blocks, 64, 1), (state_variables, blocks, 64, 8)
        )
    return expanded.reshape(state_variables, blocks, 512)


def ghost_values(own_faces, face_table, index):
    result = []
    for face_index in range(6):
        column = index[:, face_index]
        fetched = jnp.take(face_table[:, :, face_index ^ 1], jnp.maximum(column, 0), axis=1)
        selected = jnp.where(column[None, :, None] >= 0, fetched, own_faces[:, :, face_index])
        result.append(spread_face(selected, face_index // 2))
    return result


def wave_speeds(flux_derivative_matrices):
    return jnp.max(jnp.sum(jnp.abs(flux_derivative_matrices), axis=2), axis=1)


def advance(state_in, flux_derivative_matrices, speeds, rate_block, ghosts):
    position = jnp.arange(512, dtype=jnp.int32)
    change = jnp.zeros(state_in.shape, jnp.float32)
    for direction in range(3):
        stride = 64 // 8**direction
        coordinate = position // stride % 8
        lower_side = jnp.where(
            coordinate == 0, ghosts[2 * direction], jnp.roll(state_in, stride, axis=2)
        )
        upper_side = jnp.where(
            coordinate == 7, ghosts[2 * direction + 1], jnp.roll(state_in, -stride, axis=2)
        )
        difference = jnp.einsum(
            "ij,jbp->ibp",
            flux_derivative_matrices[direction],
            upper_side - lower_side,
            precision=HIGHEST_PRECISION,
        )
        change = (
            change
            + 0.5 * difference
            - 0.5 * speeds[direction] * (upper_side - 2.0 * state_in + lower_side)
        )
    return state_in - rate_block[None, :, None] * change


def shell_currents(state_in, parallel_flow_coefficients):
    state_variables, blocks = (state_in.shape[0], state_in.shape[1])
    inner_cells = state_in.reshape(state_variables, blocks, 64, 8)[:, :, :, 0:2]
    inner_cells = jnp.swapaxes(inner_cells, 2, 3).reshape(state_variables, blocks, 128)
    return jnp.einsum(
        "v,vbk->bk", parallel_flow_coefficients, inner_cells, precision=HIGHEST_PRECISION
    )


def fourier_tables(orders):
    longitudes = jnp.arange(NLON, dtype=jnp.int32)
    phase_index = longitudes[:, None] * orders[None, :] % NLON
    angle_rad = phase_index.astype(jnp.float32) * (2.0 * math.pi / NLON)
    return (jnp.cos(angle_rad), jnp.sin(angle_rad))


def legendre_start(sine_lat, orders):
    series_k = jnp.arange(1, DEGREES, dtype=jnp.int32).astype(jnp.float32)
    log_sums = jnp.concatenate(
        [
            jnp.zeros((1,), jnp.float32),
            jnp.cumsum(0.5 * jnp.log((2.0 * series_k + 1.0) / (2.0 * series_k))),
        ]
    )
    log_base = jnp.take(log_sums, orders)
    order_real = orders.astype(jnp.float32)
    return jnp.exp(
        0.5 * math.log(0.5) + log_base[None, :] + order_real[None, :] * jnp.log(sine_lat)[:, None]
    )


def legendre_next_rows(degree, orders, cosine_lat, diagonal_rows, previous, before):
    degree_real = degree.astype(jnp.float32)
    order_real = orders.astype(jnp.float32)[:, None]
    order_int = orders[:, None]
    cosine_row = cosine_lat[None, :]
    ratio_up = jnp.sqrt(
        jnp.maximum(4.0 * degree_real * degree_real - 1.0, 1.0)
        / jnp.maximum(degree_real * degree_real - order_real * order_real, 1.0)
    )
    lower_deg = degree_real - 1.0
    ratio_back = jnp.sqrt(
        jnp.maximum(lower_deg * lower_deg - order_real * order_real, 0.0)
        / jnp.maximum(4.0 * lower_deg * lower_deg - 1.0, 1.0)
    )
    coef_prev = jnp.where(
        degree == order_int + 1,
        jnp.sqrt(2.0 * order_real + 3.0) * cosine_row,
        jnp.where(degree >= order_int + 2, ratio_up * cosine_row, 0.0),
    )
    coef_before = jnp.where(degree >= order_int + 2, -ratio_up * ratio_back, 0.0)
    injected = jnp.where(degree == order_int, diagonal_rows, 0.0)
    return coef_prev * previous + coef_before * before + injected


def solve_spectral(coef_re, coef_im, cosine_lat, sine_lat, weights_lat, orders):
    diagonal_rows = jnp.transpose(legendre_start(sine_lat, orders))
    rows_re = jnp.transpose(coef_re) * weights_lat[None, :]
    rows_im = jnp.transpose(coef_im) * weights_lat[None, :]
    zero_state = jnp.zeros(diagonal_rows.shape, jnp.float32)

    def one_degree(carried, degree):
        previous, before, acc_re, acc_im = carried
        present = legendre_next_rows(degree, orders, cosine_lat, diagonal_rows, previous, before)
        spec_re = jnp.sum(rows_re * present, axis=1)
        spec_im = jnp.sum(rows_im * present, axis=1)
        degree_real = degree.astype(jnp.float32)
        gain_deg = POT_GAIN / (degree_real * (degree_real + 1.0) + KAPPA2)
        acc_re = acc_re + (gain_deg * spec_re)[:, None] * present
        acc_im = acc_im + (gain_deg * spec_im)[:, None] * present
        return ((present, previous, acc_re, acc_im), None)

    carried, _ = lax.scan(
        one_degree,
        (zero_state, zero_state, zero_state, zero_state),
        jnp.arange(DEGREES, dtype=jnp.int32),
        unroll=8,
    )
    return (jnp.transpose(carried[2]), jnp.transpose(carried[3]))


def body(
    invariant_fluid_quantities,
    flux_derivative_matrices,
    levels,
    neighbours,
    block_latitude_band,
    block_longitude_segment,
    parallel_flow_coefficients,
):
    grp_size = lax.axis_size("grp")
    core_size = lax.axis_size("cores")
    device_total = grp_size * core_size
    block_portion = invariant_fluid_quantities.shape[1]
    state_variables = invariant_fluid_quantities.shape[0]
    device = lax.axis_index(("grp", "cores"))
    speeds = wave_speeds(flux_derivative_matrices)
    rate_block = COURANT * jnp.exp2(levels.astype(jnp.float32) - (LEVELS - 1)) / jnp.max(speeds)
    offset = (device - 1) * block_portion
    local_index = jnp.where(neighbours >= 0, neighbours - offset, -1)
    parallel_flow_charge = invariant_fluid_quantities
    for section_index in range(STEPS):
        own_faces = block_faces(parallel_flow_charge)
        flat_faces = own_faces.reshape(state_variables, block_portion, 384)
        faces_prev = passed_along(flat_faces, ("grp", "cores"), 1)
        faces_next = passed_along(flat_faces, ("grp", "cores"), -1)
        face_table = jnp.concatenate([faces_prev, flat_faces, faces_next], axis=1).reshape(
            state_variables, 3 * block_portion, 6, 64
        )
        ghosts = ghost_values(own_faces, face_table, local_index)
        parallel_flow_charge = advance(
            parallel_flow_charge, flux_derivative_matrices, speeds, rate_block, ghosts
        )
    patches = shell_currents(parallel_flow_charge, parallel_flow_coefficients)
    band_index = block_latitude_band[:, 0]
    block_ids = jnp.arange(block_portion, dtype=jnp.int32)
    earlier = (band_index[None, :] == band_index[:, None]) & (
        block_ids[None, :] < block_ids[:, None]
    )
    rank_in_band = jnp.sum(earlier.astype(jnp.int32), axis=1)
    capacity = max(2, 2 * block_portion // grp_size)
    slot_index = band_index * capacity + rank_in_band
    slot_ids = jnp.arange(grp_size * capacity, dtype=jnp.int32)
    placing = (slot_ids[:, None] == slot_index[None, :]).astype(jnp.float32)
    send_rows = jnp.dot(placing, patches, precision=HIGHEST_PRECISION).reshape(
        grp_size, capacity, 128
    )
    send_codes = jnp.dot(
        placing, (block_longitude_segment + 1).astype(jnp.float32), precision=HIGHEST_PRECISION
    ).reshape(grp_size, capacity)
    got_rows, got_codes = (
        lax.all_to_all(send_rows, "grp", split_axis=0, concat_axis=0, tiled=True),
        lax.all_to_all(send_codes, "grp", split_axis=0, concat_axis=0, tiled=True),
    )
    segments = NLON // 64
    segment_codes = jnp.arange(1, segments + 1, dtype=jnp.int32).astype(jnp.float32)
    landing = (got_codes.reshape(-1)[:, None] == segment_codes[None, :]).astype(jnp.float32)
    gathered = jnp.dot(landing.T, got_rows.reshape(-1, 128), precision=HIGHEST_PRECISION)
    fac_local = jnp.swapaxes(gathered.reshape(segments, LAT_DEV, 64), 0, 1).reshape(LAT_DEV, NLON)
    orders_all = jnp.arange(DEGREES, dtype=jnp.int32)
    cos_table, sin_table = fourier_tables(orders_all)
    coef_re = jnp.dot(fac_local, cos_table, precision=HIGHEST_PRECISION) / NLON
    coef_im = -jnp.dot(fac_local, sin_table, precision=HIGHEST_PRECISION) / NLON
    lat_total = LAT_DEV * device_total
    degree_share = DEGREES // device_total
    lat_ids = jnp.arange(lat_total, dtype=jnp.int32)
    colatitude = (lat_ids.astype(jnp.float32) + 0.5) * (math.pi / lat_total)
    cosine_all = jnp.cos(colatitude)
    sine_all = jnp.sin(colatitude)
    weights_all = math.pi / lat_total * sine_all
    own_orders = device * degree_share + jnp.arange(degree_share, dtype=jnp.int32)
    stacked = jnp.stack([coef_re, coef_im])
    regrouped = lax.all_to_all(
        lax.all_to_all(stacked, "grp", split_axis=2, concat_axis=1, tiled=True),
        "cores",
        split_axis=2,
        concat_axis=1,
        tiled=True,
    )
    regrouped = jnp.transpose(
        regrouped.reshape(2, core_size, grp_size, LAT_DEV, degree_share), (0, 2, 1, 3, 4)
    ).reshape(2, lat_total, degree_share)
    synth_re, synth_im = solve_spectral(
        regrouped[0], regrouped[1], cosine_all, sine_all, weights_all, own_orders
    )
    synth_both = jnp.stack([synth_re, synth_im])
    returned = lax.all_to_all(
        lax.all_to_all(synth_both, "grp", split_axis=1, concat_axis=2, tiled=True),
        "cores",
        split_axis=1,
        concat_axis=2,
        tiled=True,
    )
    column_ids = jnp.arange(DEGREES, dtype=jnp.int32)
    order_perm = (
        degree_share
        * (
            core_size * (column_ids // degree_share % grp_size)
            + column_ids // (grp_size * degree_share)
        )
        + column_ids % degree_share
    )
    cos_perm, sin_perm = fourier_tables(order_perm)
    factor = jnp.where(order_perm == 0, jnp.float32(1.0), jnp.float32(2.0))
    potential_local = jnp.dot(
        returned[0] * factor, cos_perm.T, precision=HIGHEST_PRECISION
    ) - jnp.dot(returned[1] * factor, sin_perm.T, precision=HIGHEST_PRECISION)
    grid_segments = jnp.swapaxes(potential_local.reshape(LAT_DEV, segments, 64), 0, 1).reshape(
        segments, 128
    )
    back_rows = jnp.dot(landing, grid_segments, precision=HIGHEST_PRECISION).reshape(
        grp_size, capacity, 128
    )
    home_rows = lax.all_to_all(back_rows, "grp", split_axis=0, concat_axis=0, tiled=True)
    shell_potential = jnp.dot(placing.T, home_rows.reshape(-1, 128), precision=HIGHEST_PRECISION)
    return (parallel_flow_charge, fac_local, potential_local, shell_potential)


def solution(mesh):
    placed = (
        P(None, ("grp", "cores"), None),
        P(),
        P(("grp", "cores")),
        P(("grp", "cores"), None),
        P(("grp", "cores"), None),
        P(("grp", "cores")),
        P(),
    )
    return jax.shard_map(
        body,
        mesh=mesh,
        in_specs=placed,
        out_specs=(
            P(None, ("grp", "cores"), None),
            P(("grp", "cores"), None),
            P(("grp", "cores"), None),
            P(("grp", "cores"), None),
        ),
        check_vma=False,
    )
```

profile of v0, /device:TPU:1, one launch (start us, length us, event | category | flops | bytes accessed | tf_op | source)
XLA Modules:
  0.0 1991.3 jit_solution(3051026994790446979)
XLA Ops:
  14.9 5.1 collective-permute-start.1
  23.1 17.7 all-to-all-start
  136.1 4.4 select_subtract_fusion.3
  164.2 4.4 select_subtract_fusion.2
  192.7 5.8 broadcast_bitcast_fusion.3
  208.7 4.2 fusion.108
  234.3 3.7 copy.459
  300.4 4.4 select_subtract_fusion.1
  326.9 4.4 select_subtract_fusion
  354.8 5.8 broadcast_bitcast_fusion.1
  383.5 14.7 all-to-all-start.1
  400.4 8.9 all-to-all-done.1
  409.7 8.8 fusion.124
  418.5 8.7 fusion.115
  428.3 6.4 all-to-all-start.2
  434.7 20.4 %all-to-all-done.2 = f32[2,2,512]{1,0,2:T(2,128)S(1)} async-done(((f32[2,2,512]{1,0,2:T(2,128)}), f32[2,2,512]{1,0,2:T(2,128)S(1)}, u32[]{:S(2)}, u32[]{:S(2)}) %all-to-all-start.2) | async-done | bytes 8224 | tf_op jit(solution)/shard_map/all_to_all | solution.py:253
  462.3 1454.3 %while.23 = (s32[]{:T(128)}, f32[2,512]{1,0:T(2,128)S(1)}, f32[2,512]{1,0:T(2,128)S(1)}, f32[2,512]{1,0:T(2,128)S(1)}, f32[2,512]{1,0:T(2,128)S(1)}, /*index=5*/...) while((s32[]{:T(128)}, f32[2,512]{1,0:T(2,128)S(1)}, ...), condition=%wide.region_23.25_spmd.clone.clone.clone.clone, body=%wide.region_6.24_spmd.clone.clone.clone.clone.sunk | while | flops 140171 | bytes 140281 | solution.py:172
  1917.6 6.2 all-to-all-start.4
  1923.9 19.7 all-to-all-done.4
  1945.7 5.2 all_to_all.86
  1951.0 9.8 fusion.75
  1960.8 9.8 fusion.109
  1971.9 6.4 all-to-all-start.6
  1979.9 10.2 all-to-all-done.6
  (2674 shorter events, 1423.5 us)
Async XLA Ops:
  0.6 381.6 %copy-start = (f32[8]{0:T(128)S(1)}, f32[8]{0:T(128)}, u32[]{:S(2)}) copy-start(f32[8]{0:T(128)} %param.17) | copy-start | bytes 100
  13.4 8.5 copy-start.80
  13.4 8.7 copy-start.81
  13.5 27.4 %copy-start.1 = (f32[8,64,512]{2,1,0:T(8,128)S(1)}, f32[8,64,512]{2,1,0:T(8,128)}, u32[]{:S(2)}) copy-start(f32[8,64,512]{2,1,0:T(8,128)} %param.11) | copy-start | bytes 3145732
  14.9 98.6 %collective-permute-start.1 = (f32[8,64,384]{2,1,0:T(8,128)}, f32[8,64,384]{2,1,0:T(8,128)}, u32[]{:S(2)}, u32[]{:S(2)}) collective-permute-start(f32[8,64,384]{2,1,0:T(8,128)} %reshape.1288), channel_id=1, source_target_pairs={{1,0},{2,1},{3,2},{4,3},{5,4},{6,5},{7,6},{8,7},{9,8},{10,9},{11,1... | collective-permute-start | bytes 2359304 | tf_op jit(solution)/shard_map/ppermute | solution.py:24
  20.0 99.8 %collective-permute-start = (f32[8,64,384]{2,1,0:T(8,128)}, f32[8,64,384]{2,1,0:T(8,128)}, u32[]{:S(2)}, u32[]{:S(2)}) collective-permute-start(f32[8,64,384]{2,1,0:T(8,128)} %reshape.1288), channel_id=1, source_target_pairs={{0,1},{1,2},{2,3},{3,4},{4,5},{5,6},{6,7},{7,8},{8,9},{9,10},{10,1... | collective-permute-start | bytes 2359304 | tf_op jit(solution)/shard_map/ppermute | solution.py:24
  22.1 20.4 %copy-start.62 = (s32[64]{0:T(128)}, s32[64]{0:T(128)S(1)}, u32[]{:S(2)}) copy-start(s32[64]{0:T(128)S(1)} %multiply_add_fusion.5) | copy-start | bytes 772
  23.1 360.4 %all-to-all-start = ((f32[128,1,2]{2,1,0:T(1,128)}), f32[128,1,2]{2,1,0:T(1,128)S(1)}, u32[]{:S(2)}, u32[]{:S(2)}) async-start(f32[128,1,2]{2,1,0:T(1,128)} %bitcast.104), calls=%async_computation | async-start | bytes 131072 | tf_op jit(solution)/shard_map/all_to_all | solution.py:232
  58.1 7.0 copy-start.47
  58.1 7.8 copy-start.23
  126.9 7.8 copy-start.58
  150.0 10.5 copy-start.57
  240.7 38.1 %collective-permute-start.3 = (f32[8,64,384]{2,1,0:T(8,128)}, f32[8,64,384]{2,1,0:T(8,128)}, u32[]{:S(2)}, u32[]{:S(2)}) collective-permute-start(f32[8,64,384]{2,1,0:T(8,128)} %reshape.1296), channel_id=1, source_target_pairs={{1,0},{2,1},{3,2},{4,3},{5,4},{6,5},{7,6},{8,7},{9,8},{10,9},{11,1... | collective-permute-start | bytes 2359304 | tf_op jit(solution)/shard_map/ppermute | solution.py:24
  242.6 42.5 %collective-permute-start.2 = (f32[8,64,384]{2,1,0:T(8,128)}, f32[8,64,384]{2,1,0:T(8,128)}, u32[]{:S(2)}, u32[]{:S(2)}) collective-permute-start(f32[8,64,384]{2,1,0:T(8,128)} %reshape.1296), channel_id=1, source_target_pairs={{0,1},{1,2},{2,3},{3,4},{4,5},{5,6},{6,7},{7,8},{8,9},{9,10},{10,1... | collective-permute-start | bytes 2359304 | tf_op jit(solution)/shard_map/ppermute | solution.py:24
  342.1 7.5 copy-start.56
  342.1 7.5 copy-start.59
  342.1 7.5 copy-start.60
  383.5 25.8 %all-to-all-start.1 = ((f32[128,2,128]{2,1,0:T(2,128)}), f32[128,2,128]{2,1,0:T(2,128)S(1)}, u32[]{:S(2)}, u32[]{:S(2)}) async-start(f32[128,2,128]{2,1,0:T(2,128)} %bitcast.111), calls=%async_computation.1 | async-start | bytes 262144 | tf_op jit(solution)/shard_map/all_to_all | solution.py:231
  409.7 8.8 copy-start.53
  428.3 26.9 %all-to-all-start.2 = ((f32[2,2,512]{1,0,2:T(2,128)}), f32[2,2,512]{1,0,2:T(2,128)S(1)}, u32[]{:S(2)}, u32[]{:S(2)}) async-start(f32[2,2,512]{1,0,2:T(2,128)} %copy.486), calls=%async_computation.2 | async-start | bytes 1048576 | tf_op jit(solution)/shard_map/all_to_all | solution.py:253
  1916.6 34.4 %copy-start.78 = (s32[512]{0:T(512)S(1)}, s32[512]{0:T(512)}, u32[]{:S(2)}) copy-start(s32[512]{0:T(512)} %fusion.182) | copy-start | bytes 6148
  1917.6 26.0 %all-to-all-start.4 = ((f32[2,512,2]{2,0,1:T(2,128)}), f32[2,512,2]{2,0,1:T(2,128)S(1)}, u32[]{:S(2)}, u32[]{:S(2)}) async-start(f32[2,512,2]{2,0,1:T(2,128)} %copy.493), calls=%async_computation.4 | async-start | bytes 1048576 | tf_op jit(solution)/shard_map/all_to_all | solution.py:267
  1970.6 20.4 %copy-start.54 = (f32[2,1024]{1,0:T(2,128)}, f32[2,1024]{1,0:T(2,128)S(1)}, u32[]{:S(2)}) copy-start(f32[2,1024]{1,0:T(2,128)S(1)} %fusion.109) | copy-start | bytes 24580
  1971.9 18.2 all-to-all-start.6
  (67 other events, 212.2 us)
where the time goes:
time: 2020 us; the launch traced here: 1990 us
  other arithmetic  1110 us (55%)
  loops' own time  368 us (18%)
  local copies, waits for them, and re-layouts  316 us (16%)
  starting transfers between devices  64 us (3%)
  waiting for transfers between devices  59.2 us (3%)
  matrix products  56.1 us (3%)
    another operation x1, loops' own time, solve_spectral(): lax.scan(one_degree, (zero_state, zero_state, zero_state, zero_state), jn...  368 us
    select_n x256, other arithmetic, legendre_next_rows(): jnp.where(degree >= order_int + 2, -ratio_up * ratio_back, 0.0)  328 us
    eq x256, other arithmetic, legendre_next_rows(): degree == order_int + 1  325 us
    eq x256, other arithmetic, legendre_next_rows(): injected = jnp.where(degree == order_int, diagonal_rows, 0.0)  324 us
    reduce_sum x64, other arithmetic, one_degree(): spec_im = jnp.sum(rows_im * present, axis=1)  43 us
  transfers between devices with their start and end apart: 9, of which 4 were waited for; matrix products, arithmetic and copies ran while one was open for 17% of the time, Pallas kernels for 0%

commit v1 on v0

v1 whole, which is shorter than its diff:
```python
import functools
import math

import jax
import jax.numpy as jnp
from jax import lax
from jax.experimental import pallas as pl
from jax.experimental.pallas import tpu as pltpu
from jax.sharding import PartitionSpec as P

LEVELS = 4
STEPS = 2
LAT_DEV = 2
NLON = 1024
DEGREES = 512


COURANT = 0.3
KAPPA2 = 400.0
POT_GAIN = 2000.0
HIGHEST_PRECISION = lax.Precision.HIGHEST


def passed_along(value, axis, steps):
    count = lax.axis_size(axis)
    leading, last = (max(0, -steps), min(count, count - steps))
    return lax.ppermute(value, axis, [(source, source + steps) for source in range(leading, last)])


def iota(shape, dim):
    return lax.broadcasted_iota(jnp.int32, shape, dim)


def face_selection():
    cell, col = iota((512, 256), 0), iota((512, 256), 1)
    face, c = col // 64, col % 64
    along_y = 64 * (c // 8) + jnp.where(face == 0, 56, 0) + c % 8
    along_z = 64 * (c // 8) + 8 * (c % 8) + jnp.where(face == 2, 7, 0)
    return (cell == jnp.where(face < 2, along_y, along_z)).astype(jnp.bfloat16)


def ghost_expansion():
    shape = (2, 256, 512)
    along, row, cell = iota(shape, 0), iota(shape, 1) % 128, iota(shape, 2)
    c, top = row % 64, row // 64
    target_y = 64 * (c // 8) + 56 * top + c % 8
    target_z = 64 * (c // 8) + 8 * (c % 8) + 7 * top
    return (cell == jnp.where(along == 0, target_y, target_z)).astype(jnp.bfloat16)


def patch_selection():
    cell, k = iota((512, 128), 0), iota((512, 128), 1)
    return (cell == 8 * (k % 64) + k // 64).astype(jnp.bfloat16)


def split_two(value):
    high = value.astype(jnp.bfloat16)
    return high, (value - high.astype(jnp.float32)).astype(jnp.bfloat16)


def product(left, right):
    return jnp.dot(left, right, preferred_element_type=jnp.float32)


def write_faces(state_ref, select_ref, faces_ref):
    first_half = iota((64, 128), 1) < 64
    selection = select_ref[...]
    for v in range(state_ref.shape[0]):
        head = pltpu.roll(state_ref[v, :, 0:128], 64, 1)
        tail = pltpu.roll(state_ref[v, :, 384:512], 64, 1)
        faces_ref[v, :, 0:128] = jnp.where(first_half, tail, head)
        high, low = split_two(state_ref[v])
        faces_ref[v, :, 128:384] = product(high, selection) + product(low, selection)


def faces_kernel(state_ref, select_ref, faces_ref):
    write_faces(state_ref, select_ref, faces_ref)


def step_kernel(
    mix_ref,
    speed_ref,
    flow_ref,
    state_ref,
    prev_ref,
    own_ref,
    next_ref,
    pick_ref,
    expand_ref,
    rate_ref,
    select_ref,
    out_ref,
    extra_ref,
    ghost_ref,
    spread_ref,
    gx_ref,
    last,
):
    variables = state_ref.shape[0]
    first_half = iota((64, 128), 1) < 64
    for d in range(3):
        lanes = slice(128 * d, 128 * d + 128)
        for v in range(variables):
            own = own_ref[v, :, lanes]
            table = jnp.concatenate(
                [prev_ref[v, :, lanes], own, next_ref[v, :, lanes], pltpu.roll(own, 64, 1)], axis=0
            )
            both = product(pick_ref[d], jnp.concatenate(split_two(table), axis=1))
            high = jnp.where(first_half, both[0:64, 0:128], both[64:128, 0:128])
            low = jnp.where(first_half, both[0:64, 128:256], both[64:128, 128:256])
            if d == 0:
                gx_ref[v] = high + low
            else:
                ghost_ref[d - 1, pl.ds(64 * v, 64), 0:128] = high.astype(jnp.bfloat16)
                ghost_ref[d - 1, pl.ds(64 * v, 64), 128:256] = low.astype(jnp.bfloat16)
    for d in range(2):
        spread_ref[d] = product(ghost_ref[d], expand_ref[d])

    lane = iota((8, 128), 1)
    lower_half = lane < 64
    y_low, y_top = lane // 8 % 8 == 0, lane // 8 % 8 == 7
    z_low, z_top = lane % 8 == 0, lane % 8 == 7

    def rows_step(group, carry):
        start = pl.multiple_of(8 * group, 8)
        rows = pl.ds(start, 8)
        rate = rate_ref[rows, :]
        for chunk in range(4):
            lanes = slice(128 * chunk, 128 * chunk + 128)
            diffs, values, smooth = [[], [], []], [], []
            for v in range(variables):
                u = state_ref[v, rows, lanes]
                middle = pltpu.roll(u, 64, 1)
                if chunk > 0:
                    below = pltpu.roll(state_ref[v, rows, 128 * chunk - 128 : 128 * chunk], 64, 1)
                else:
                    below = gx_ref[v, rows, :]
                if chunk < 3:
                    above = pltpu.roll(state_ref[v, rows, 128 * chunk + 128 : 128 * chunk + 256], 64, 1)
                else:
                    above = gx_ref[v, rows, :]
                spread_rows = pl.ds(pl.multiple_of(64 * v + start, 8), 8)
                gy = spread_ref[0, spread_rows, lanes]
                gz = spread_ref[1, spread_rows, lanes]
                pairs = [
                    (jnp.where(lower_half, below, middle), jnp.where(lower_half, middle, above)),
                    (
                        jnp.where(y_low, gy, pltpu.roll(u, 8, 1)),
                        jnp.where(y_top, gy, pltpu.roll(u, 120, 1)),
                    ),
                    (
                        jnp.where(z_low, gz, pltpu.roll(u, 1, 1)),
                        jnp.where(z_top, gz, pltpu.roll(u, 127, 1)),
                    ),
                ]
                twice = u + u
                total = None
                for d in range(3):
                    lower, upper = pairs[d]
                    diffs[d].append(upper - lower)
                    term = speed_ref[d] * ((upper - twice) + lower)
                    total = term if total is None else total + term
                values.append(u)
                smooth.append(total)
            for i in range(variables):
                change = -smooth[i]
                for d in range(3):
                    for j in range(variables):
                        change = change + mix_ref[64 * d + 8 * i + j] * diffs[d][j]
                out_ref[i, rows, lanes] = values[i] - rate * change
        return carry

    lax.fori_loop(0, 8, rows_step, 0)
    if last:
        total = flow_ref[0] * out_ref[0]
        for v in range(1, variables):
            total = total + flow_ref[v] * out_ref[v]
        high, rest = total.astype(jnp.bfloat16), None
        rest = total - high.astype(jnp.float32)
        middle, low = split_two(rest)
        selection = select_ref[...]
        extra_ref[...] = product(high, selection) + (
            product(middle, selection) + product(low, selection)
        )
    else:
        write_faces(out_ref, select_ref, extra_ref)


SMEM_SPEC = pl.BlockSpec(memory_space=pltpu.SMEM)
VMEM_SPEC = pl.BlockSpec(memory_space=pltpu.VMEM)
INTERPRET = False


def make_faces(state_in, selection):
    return pl.pallas_call(
        faces_kernel,
        out_shape=jax.ShapeDtypeStruct(state_in.shape[:2] + (384,), jnp.float32),
        in_specs=[VMEM_SPEC] * 2,
        out_specs=VMEM_SPEC,
        interpret=INTERPRET,
    )(state_in, selection)


def advance(mix, speeds, flow, state_in, prev, own, following, pick, expand, rate, selection, last):
    variables, blocks = state_in.shape[:2]
    extra = (blocks, 128) if last else (variables, blocks, 384)
    return pl.pallas_call(
        functools.partial(step_kernel, last=last),
        out_shape=(
            jax.ShapeDtypeStruct(state_in.shape, jnp.float32),
            jax.ShapeDtypeStruct(extra, jnp.float32),
        ),
        in_specs=[SMEM_SPEC] * 3 + [VMEM_SPEC] * 8,
        out_specs=(VMEM_SPEC, VMEM_SPEC),
        scratch_shapes=[
            pltpu.VMEM((2, 64 * variables, 256), jnp.bfloat16),
            pltpu.VMEM((2, 64 * variables, 512), jnp.float32),
            pltpu.VMEM((variables, 64, 128), jnp.float32),
        ],
        interpret=INTERPRET,
    )(mix, speeds, flow, state_in, prev, own, following, pick, expand, rate, selection)


def block_picks(neighbours, offset):
    blocks = neighbours.shape[0]
    local = jnp.where(
        neighbours >= 0, neighbours - offset, 3 * blocks + jnp.arange(blocks, dtype=jnp.int32)[:, None]
    )
    index = jnp.transpose(local).reshape(3, 2 * blocks)
    return (index[:, :, None] == iota((3, 2 * blocks, 4 * blocks), 2)).astype(jnp.bfloat16)


def wave_speeds(flux_derivative_matrices):
    return jnp.max(jnp.sum(jnp.abs(flux_derivative_matrices), axis=2), axis=1)


def fourier_tables(orders):
    longitudes = jnp.arange(NLON, dtype=jnp.int32)
    phase_index = longitudes[:, None] * orders[None, :] % NLON
    angle_rad = phase_index.astype(jnp.float32) * (2.0 * math.pi / NLON)
    return (jnp.cos(angle_rad), jnp.sin(angle_rad))


def legendre_start(sine_lat, orders):
    series_k = jnp.arange(1, DEGREES, dtype=jnp.int32).astype(jnp.float32)
    log_sums = jnp.concatenate(
        [
            jnp.zeros((1,), jnp.float32),
            jnp.cumsum(0.5 * jnp.log((2.0 * series_k + 1.0) / (2.0 * series_k))),
        ]
    )
    log_base = jnp.take(log_sums, orders)
    order_real = orders.astype(jnp.float32)
    return jnp.exp(
        0.5 * math.log(0.5) + log_base[None, :] + order_real[None, :] * jnp.log(sine_lat)[:, None]
    )


def recurrence_factors(orders):
    degree = iota((DEGREES, orders.shape[0]), 0)
    order = jnp.broadcast_to(orders[None, :], degree.shape)
    degree_real, order_real = degree.astype(jnp.float32), order.astype(jnp.float32)
    ratio_up = jnp.sqrt(
        jnp.maximum(4.0 * degree_real * degree_real - 1.0, 1.0)
        / jnp.maximum(degree_real * degree_real - order_real * order_real, 1.0)
    )
    lower_deg = degree_real - 1.0
    ratio_back = jnp.sqrt(
        jnp.maximum(lower_deg * lower_deg - order_real * order_real, 0.0)
        / jnp.maximum(4.0 * lower_deg * lower_deg - 1.0, 1.0)
    )
    coef_prev = jnp.where(
        degree == order + 1,
        jnp.sqrt(2.0 * order_real + 3.0),
        jnp.where(degree >= order + 2, ratio_up, 0.0),
    )
    coef_before = jnp.where(degree >= order + 2, -ratio_up * ratio_back, 0.0)
    return coef_prev, coef_before


def spectral_kernel(
    first_ref, prev_ref, before_ref, gain_ref, re_ref, im_ref, diagonal_ref, cosine_ref, out_re, out_im
):
    even = iota((8, 128), 0) % 2 == 0
    order = first_ref[0] + iota((8, 128), 0) % 2
    rows_re, rows_im = re_ref[...], im_ref[...]
    diagonal, cosine = diagonal_ref[...], cosine_ref[...]
    zero = jnp.zeros((8, 128), jnp.float32)

    def over_latitudes(value):
        value = value + pltpu.roll(value, 4, 0)
        value = value + pltpu.roll(value, 2, 0)
        return jnp.sum(value, axis=1, keepdims=True)

    def some_degrees(step, carried):
        previous, before, acc_re, acc_im = carried
        for inner in range(16):
            degree = 16 * step + inner
            up = jnp.where(even, prev_ref[2 * degree], prev_ref[2 * degree + 1])
            back = jnp.where(even, before_ref[2 * degree], before_ref[2 * degree + 1])
            present = (up * cosine) * previous + back * before
            present = jnp.where(order == degree, diagonal, present)
            gain = gain_ref[degree]
            acc_re = acc_re + (gain * over_latitudes(rows_re * present)) * present
            acc_im = acc_im + (gain * over_latitudes(rows_im * present)) * present
            previous, before = present, previous
        return previous, before, acc_re, acc_im

    carried = lax.fori_loop(0, DEGREES // 16, some_degrees, (zero, zero, zero, zero))
    out_re[...] = carried[2]
    out_im[...] = carried[3]


def solve_spectral(coef_re, coef_im, cosine_lat, sine_lat, weights_lat, orders):
    def folded(rows):
        return jnp.swapaxes(rows.reshape(2, 4, 128), 0, 1).reshape(8, 128)

    def unfolded(value):
        return jnp.swapaxes(value.reshape(4, 2, 128), 0, 1).reshape(2, 512)

    diagonal = folded(jnp.transpose(legendre_start(sine_lat, orders)))
    coef_prev, coef_before = recurrence_factors(orders)
    degree_real = jnp.arange(DEGREES, dtype=jnp.int32).astype(jnp.float32)
    gain = POT_GAIN / (degree_real * (degree_real + 1.0) + KAPPA2)
    shape = jax.ShapeDtypeStruct((8, 128), jnp.float32)
    acc_re, acc_im = pl.pallas_call(
        spectral_kernel,
        out_shape=(shape, shape),
        in_specs=[SMEM_SPEC] * 4 + [VMEM_SPEC] * 4,
        out_specs=(VMEM_SPEC, VMEM_SPEC),
        interpret=INTERPRET,
    )(
        orders[0:1],
        coef_prev.reshape(-1),
        coef_before.reshape(-1),
        gain,
        folded(coef_re * weights_lat[None, :]),
        folded(coef_im * weights_lat[None, :]),
        diagonal,
        folded(jnp.broadcast_to(cosine_lat[None, :], (2, 512))),
    )
    return unfolded(acc_re), unfolded(acc_im)


def body(
    invariant_fluid_quantities,
    flux_derivative_matrices,
    levels,
    neighbours,
    block_latitude_band,
    block_longitude_segment,
    parallel_flow_coefficients,
):
    grp_size = lax.axis_size("grp")
    core_size = lax.axis_size("cores")
    device_total = grp_size * core_size
    block_portion = invariant_fluid_quantities.shape[1]
    state_variables = invariant_fluid_quantities.shape[0]
    device = lax.axis_index(("grp", "cores"))
    speeds = wave_speeds(flux_derivative_matrices)
    rate_block = COURANT * jnp.exp2(levels.astype(jnp.float32) - (LEVELS - 1)) / jnp.max(speeds)
    offset = (device - 1) * block_portion
    picks = block_picks(neighbours, offset)
    selection, expand = face_selection(), ghost_expansion()
    rate = jnp.broadcast_to(rate_block[:, None], (block_portion, 128))
    mix = 0.5 * flux_derivative_matrices.reshape(-1)
    half_speeds = 0.5 * speeds
    parallel_flow_charge = invariant_fluid_quantities
    faces = make_faces(parallel_flow_charge, selection)
    for section_index in range(STEPS):
        last = section_index == STEPS - 1
        parallel_flow_charge, faces = advance(
            mix,
            half_speeds,
            parallel_flow_coefficients,
            parallel_flow_charge,
            passed_along(faces, ("grp", "cores"), 1),
            faces,
            passed_along(faces, ("grp", "cores"), -1),
            picks,
            expand,
            rate,
            patch_selection() if last else selection,
            last,
        )
    patches = faces
    band_index = block_latitude_band[:, 0]
    block_ids = jnp.arange(block_portion, dtype=jnp.int32)
    earlier = (band_index[None, :] == band_index[:, None]) & (
        block_ids[None, :] < block_ids[:, None]
    )
    rank_in_band = jnp.sum(earlier.astype(jnp.int32), axis=1)
    capacity = max(2, 2 * block_portion // grp_size)
    slot_index = band_index * capacity + rank_in_band
    slot_ids = jnp.arange(grp_size * capacity, dtype=jnp.int32)
    placing = (slot_ids[:, None] == slot_index[None, :]).astype(jnp.float32)
    send_rows = jnp.dot(placing, patches, precision=HIGHEST_PRECISION).reshape(
        grp_size, capacity, 128
    )
    send_codes = jnp.dot(
        placing, (block_longitude_segment + 1).astype(jnp.float32), precision=HIGHEST_PRECISION
    ).reshape(grp_size, capacity)
    got_rows, got_codes = (
        lax.all_to_all(send_rows, "grp", split_axis=0, concat_axis=0, tiled=True),
        lax.all_to_all(send_codes, "grp", split_axis=0, concat_axis=0, tiled=True),
    )
    segments = NLON // 64
    segment_codes = jnp.arange(1, segments + 1, dtype=jnp.int32).astype(jnp.float32)
    landing = (got_codes.reshape(-1)[:, None] == segment_codes[None, :]).astype(jnp.float32)
    gathered = jnp.dot(landing.T, got_rows.reshape(-1, 128), precision=HIGHEST_PRECISION)
    fac_local = jnp.swapaxes(gathered.reshape(segments, LAT_DEV, 64), 0, 1).reshape(LAT_DEV, NLON)
    orders_all = jnp.arange(DEGREES, dtype=jnp.int32)
    cos_table, sin_table = fourier_tables(orders_all)
    coef_re = jnp.dot(fac_local, cos_table, precision=HIGHEST_PRECISION) / NLON
    coef_im = -jnp.dot(fac_local, sin_table, precision=HIGHEST_PRECISION) / NLON
    lat_total = LAT_DEV * device_total
    degree_share = DEGREES // device_total
    lat_ids = jnp.arange(lat_total, dtype=jnp.int32)
    colatitude = (lat_ids.astype(jnp.float32) + 0.5) * (math.pi / lat_total)
    cosine_all = jnp.cos(colatitude)
    sine_all = jnp.sin(colatitude)
    weights_all = math.pi / lat_total * sine_all
    own_orders = device * degree_share + jnp.arange(degree_share, dtype=jnp.int32)
    stacked = jnp.stack([coef_re, coef_im])
    regrouped = lax.all_to_all(
        lax.all_to_all(stacked, "grp", split_axis=2, concat_axis=1, tiled=True),
        "cores",
        split_axis=2,
        concat_axis=1,
        tiled=True,
    )
    regrouped = jnp.transpose(
        regrouped.reshape(2, core_size, grp_size, LAT_DEV, degree_share), (0, 2, 1, 3, 4)
    ).reshape(2, lat_total, degree_share)
    synth_re, synth_im = solve_spectral(
        jnp.transpose(regrouped[0]),
        jnp.transpose(regrouped[1]),
        cosine_all,
        sine_all,
        weights_all,
        own_orders,
    )
    synth_both = jnp.stack([jnp.transpose(synth_re), jnp.transpose(synth_im)])
    returned = lax.all_to_all(
        lax.all_to_all(synth_both, "grp", split_axis=1, concat_axis=2, tiled=True),
        "cores",
        split_axis=1,
        concat_axis=2,
        tiled=True,
    )
    column_ids = jnp.arange(DEGREES, dtype=jnp.int32)
    order_perm = (
        degree_share
        * (
            core_size * (column_ids // degree_share % grp_size)
            + column_ids // (grp_size * degree_share)
        )
        + column_ids % degree_share
    )
    cos_perm, sin_perm = fourier_tables(order_perm)
    factor = jnp.where(order_perm == 0, jnp.float32(1.0), jnp.float32(2.0))
    potential_local = jnp.dot(
        returned[0] * factor, cos_perm.T, precision=HIGHEST_PRECISION
    ) - jnp.dot(returned[1] * factor, sin_perm.T, precision=HIGHEST_PRECISION)
    grid_segments = jnp.swapaxes(potential_local.reshape(LAT_DEV, segments, 64), 0, 1).reshape(
        segments, 128
    )
    back_rows = jnp.dot(landing, grid_segments, precision=HIGHEST_PRECISION).reshape(
        grp_size, capacity, 128
    )
    home_rows = lax.all_to_all(back_rows, "grp", split_axis=0, concat_axis=0, tiled=True)
    shell_potential = jnp.dot(placing.T, home_rows.reshape(-1, 128), precision=HIGHEST_PRECISION)
    return (parallel_flow_charge, fac_local, potential_local, shell_potential)


def solution(mesh):
    placed = (
        P(None, ("grp", "cores"), None),
        P(),
        P(("grp", "cores")),
        P(("grp", "cores"), None),
        P(("grp", "cores"), None),
        P(("grp", "cores")),
        P(),
    )
    return jax.shard_map(
        body,
        mesh=mesh,
        in_specs=placed,
        out_specs=(
            P(None, ("grp", "cores"), None),
            P(("grp", "cores"), None),
            P(("grp", "cores"), None),
            P(("grp", "cores"), None),
        ),
        check_vma=False,
    )
```

time: 2020 us -> 252 us (0.12); the launches traced: 1990 us -> 248 us
  other arithmetic: 1110 us -> 10.6 us
  loops' own time: 368 us -> 0 us
  local copies, waits for them, and re-layouts: 316 us -> 16.7 us
  Pallas kernels: 0 us -> 26.8 us
    eq x524 -> x2, other arithmetic: 655 us -> 0.05 us  [the longest x1 0.05 us: recurrence_factors(): degree == order + 1]
    another operation x1 -> x0, loops' own time: 368 us -> none  [solve_spectral(): lax.scan(one_degree, (zero_state, zero_state, zero_state, zero_state), jn...]
    select_n x266 -> x1, other arithmetic: 344 us -> 0.61 us  [recurrence_factors(): coef_before = jnp.where(degree >= order + 2, -ratio_up * ratio_back, 0.0)]
    concatenate x20 -> x0, local copies, waits for them, and re-layouts: 56.2 us -> none  [the longest x8 23.3 us: body(): jnp.concatenate([faces_prev, flat_faces, faces_next], axis=1)]
    slice x79 -> x1, local copies, waits for them, and re-layouts: 54.4 us -> 0.07 us  [the longest x64 39.7 us: solve_spectral(): lax.scan(one_degree, (zero_state, zero_state, zero_state, zero_state), jn...]
    reshape x17 -> x3, local copies, waits for them, and re-layouts: 44.6 us -> 0.03 us  [the longest x2 0.03 us: folded(): return jnp.swapaxes(rows.reshape(2, 4, 128), 0, 1).reshape(8, 128)]
    reduce_sum x64 -> x0, other arithmetic: 43 us -> none  [one_degree(): spec_im = jnp.sum(rows_im * present, axis=1)]
    another operation x35 -> x2, local copies, waits for them, and re-layouts: 37 us -> 1.16 us  [the longest x1 1.04 us: body(): synth_both = jnp.stack([jnp.transpose(synth_re), jnp.transpose(synth_im)])]
  transfers between devices with their start and end apart: 9 -> 8, of which waited for: 4 -> 5; matrix products, arithmetic and copies ran while one was open for 17% -> 6% of each run, Pallas kernels for 0% -> 7%
where the time goes in v1:
time: 252 us; the launch traced here: 248 us
  starting transfers between devices  65.8 us (26%)
  waiting for transfers between devices  58.8 us (23%)
  matrix products  40.3 us (16%)
  blocking collectives  27.8 us (11%)
  Pallas kernels  26.8 us (11%)
  local copies, waits for them, and re-layouts  16.7 us (7%)
  other arithmetic  10.6 us (4%)
    all_to_all x1, waiting for transfers between devices, body(): lax.all_to_all(stacked, 'grp', split_axis=2, concat_axis=1, tiled=True)  19.8 us
    all_to_all x1, waiting for transfers between devices, body(): lax.all_to_all(synth_both, 'grp', split_axis=1, concat_axis=2, tiled=True)  19.7 us
    all_to_all x1, blocking collectives, body(): lax.all_to_all(back_rows, 'grp', split_axis=0, concat_axis=0, tiled=True)  17.3 us
    pallas_call x2, Pallas kernels, advance(): pl.pallas_call(functools.partial(step_kernel, last=last), out_shape=(jax....  17.3 us
    all_to_all x1, starting transfers between devices, body(): lax.all_to_all(stacked, 'grp', split_axis=2, concat_axis=1, tiled=True)  15.9 us
    all_to_all x1, starting transfers between devices, body(): lax.all_to_all(send_rows, 'grp', split_axis=0, concat_axis=0, tiled=True)  15.1 us
    all_to_all x1, starting transfers between devices, body(): lax.all_to_all(send_codes, 'grp', split_axis=0, concat_axis=0, tiled=True)  14.6 us
    ppermute x4, starting transfers between devices, passed_along(): lax.ppermute(value, axis, [(source, source + steps) for source in range(l...  14 us
  transfers between devices with their start and end apart: 8, of which 5 were waited for; matrix products, arithmetic and copies ran while one was open for 6% of the time, Pallas kernels for 7%

profile of v1, /device:TPU:1, one launch (start us, length us, event | category | flops | bytes accessed | tf_op | source)
XLA Modules:
  0.0 248.1 jit_solution(2906503792408271062)
XLA Ops:
  1.5 3.0 %shard_map.102.own_ref = f32[8,64,384]{2,1,0:T(8,128)} custom-call(f32[8,64,512]{2,1,0:T(8,128)} %state_ref.3, bf16[512,256]{1,0:T(8,128)(2,1)} %fusion.57.select_ref), custom_call_target="tpu_custom_call" | custom-call | tf_op jit(solution)/shard_map/pallas_call | solution.py:195
  4.5 4.9 %collective-permute-start = (f32[8,64,384]{2,1,0:T(8,128)}, f32[8,64,384]{2,1,0:T(8,128)S(1)}, u32[]{:S(2)}, u32[]{:S(2)}) collective-permute-start(f32[8,64,384]{2,1,0:T(8,128)} %shard_map.102.own_ref), channel_id=1, source_target_pairs={{0,1},{1,2},{2,3},{3,4},{4,5},{5,6},{6,7},{7,8},{8,9},{9,10},{10,1... | collective-permute-start | bytes 2359304 | tf_op jit(solution)/shard_map/ppermute | solution.py:27
  9.4 1.9 collective-permute-start.1
  12.5 14.6 %all-to-all-start = ((f32[128,1,2]{2,1,0:T(1,128)}), f32[128,1,2]{2,1,0:T(1,128)S(1)}, u32[]{:S(2)}, u32[]{:S(2)}) async-start(f32[128,1,2]{2,1,0:T(1,128)} %bitcast.4), calls=%async_computation | async-start | bytes 131072 | tf_op jit(solution)/shard_map/all_to_all | solution.py:405
  36.4 9.0 %shard_map.103 = (f32[8,64,512]{2,1,0:T(8,128)}, f32[8,64,384]{2,1,0:T(8,128)}) custom-call(f32[192]{0:T(256)} %mul.305.mix_ref, f32[3]{0:T(128)} %broadcast_multiply_fusion.1.speed_ref, f32[8]{0:T(128)} %flow_ref.3, f32[8,64,512]{2,1,0:T(8,128)} %state_ref.3, f32[8,64,384]{2,1,0:T(8,128)} %copy-done, f32[8,64,384]{2,1,0:T(8,128)} %shard_map.102.own_ref, ...), custom_call_target="tpu_custom_call" | custom-call | tf_op jit(solution)/shard_map/pallas_call | solution.py:207
  45.4 5.2 %collective-permute-start.2 = (f32[8,64,384]{2,1,0:T(8,128)}, f32[8,64,384]{2,1,0:T(8,128)S(1)}, u32[]{:S(2)}, u32[]{:S(2)}) collective-permute-start(f32[8,64,384]{2,1,0:T(8,128)} %get-tuple-element.11.own_ref), channel_id=1, source_target_pairs={{0,1},{1,2},{2,3},{3,4},{4,5},{5,6},{6,7},{7,8},{8,9},{9,10},{10,1... | collective-permute-start | bytes 2359304 | tf_op jit(solution)/shard_map/ppermute | solution.py:27
  50.7 1.9 collective-permute-start.3
  53.9 6.0 %collective-permute-done.2.prev_ref = f32[8,64,384]{2,1,0:T(8,128)S(1)} collective-permute-done((f32[8,64,384]{2,1,0:T(8,128)}, f32[8,64,384]{2,1,0:T(8,128)S(1)}, u32[]{:S(2)}, u32[]{:S(2)}) %collective-permute-start.2) | collective-permute-done | bytes 786464 | tf_op jit(solution)/shard_map/ppermute | solution.py:27
  59.9 4.3 %collective-permute-done.3.next_ref = f32[8,64,384]{2,1,0:T(8,128)S(1)} collective-permute-done((f32[8,64,384]{2,1,0:T(8,128)}, f32[8,64,384]{2,1,0:T(8,128)S(1)}, u32[]{:S(2)}, u32[]{:S(2)}) %collective-permute-start.3) | collective-permute-done | bytes 786464 | tf_op jit(solution)/shard_map/ppermute | solution.py:27
  65.1 8.2 %shard_map.104 = (f32[8,64,512]{2,1,0:T(8,128)}, f32[64,128]{1,0:T(8,128)}) custom-call(f32[192]{0:T(256)} %mul.305.mix_ref, f32[3]{0:T(128)} %broadcast_multiply_fusion.1.speed_ref, f32[8]{0:T(128)} %flow_ref.3, f32[8,64,512]{2,1,0:T(8,128)} %get-tuple-element.10.state_ref, f32[8,64,384]{2,1,0:T(8,128)} %copy-done.2, ...), custom_call_target="tpu_custom_call" | custom-call | tf_op jit(solution)/shard_map/pallas_call | solution.py:207
  74.9 15.1 %all-to-all-start.1 = ((f32[128,2,128]{2,1,0:T(2,128)}), f32[128,2,128]{2,1,0:T(2,128)S(1)}, u32[]{:S(2)}, u32[]{:S(2)}) async-start(f32[128,2,128]{2,1,0:T(2,128)} %bitcast.6), calls=%async_computation.1 | async-start | bytes 262144 | tf_op jit(solution)/shard_map/all_to_all | solution.py:404
  93.3 9.0 %all-to-all-done.1 = f32[128,2,128]{2,1,0:T(2,128)S(1)} async-done(((f32[128,2,128]{2,1,0:T(2,128)}), f32[128,2,128]{2,1,0:T(2,128)S(1)}, u32[]{:S(2)}, u32[]{:S(2)}) %all-to-all-start.1) | async-done | bytes 131104 | tf_op jit(solution)/shard_map/all_to_all | solution.py:404
  102.8 8.7 %fusion.26 = f32[1,2,512]{2,1,0:T(2,128)S(1)} fusion(f32[2,1024]{1,0:T(2,128)S(1)} %reshape.301), kind=kOutput, calls=%fused_computation.47 | convolution fusion | flops 19923968 | bytes 12288 | tf_op jit(solution)/shard_map/dot_general | solution.py:414
  111.5 8.8 %fusion.35 = f32[1,2,512]{2,1,0:T(2,128)S(1)} fusion(f32[2,1024]{1,0:T(2,128)S(1)} %reshape.301), kind=kOutput, calls=%fused_computation.50 | convolution fusion | flops 19924992 | bytes 12288 | tf_op jit(solution)/shard_map/dot_general | solution.py:415
  121.4 15.9 %all-to-all-start.2 = ((f32[2,2,512]{1,0,2:T(2,128)}), f32[2,2,512]{1,0,2:T(2,128)S(1)}, u32[]{:S(2)}, u32[]{:S(2)}) async-start(f32[2,2,512]{1,0,2:T(2,128)} %copy.103), calls=%async_computation.2 | async-start | bytes 1048576 | tf_op jit(solution)/shard_map/all_to_all | solution.py:426
  137.3 19.8 %all-to-all-done.2 = f32[2,2,512]{1,0,2:T(2,128)S(1)} async-done(((f32[2,2,512]{1,0,2:T(2,128)}), f32[2,2,512]{1,0,2:T(2,128)S(1)}, u32[]{:S(2)}, u32[]{:S(2)}) %all-to-all-start.2) | async-done | bytes 8224 | tf_op jit(solution)/shard_map/all_to_all | solution.py:426
  159.2 5.2 %all_to_all.85 = f32[2,256,4]{1,0,2:T(2,128)S(1)} all-to-all(f32[2,256,4]{1,0,2:T(2,128)S(1)} %copy.106), channel_id=1, replica_groups=mesh['grp'=128,'cores'=2] {'cores'}, dimensions={2} | all-to-all | bytes 16384 | tf_op jit(solution)/shard_map/all_to_all | solution.py:425
  167.8 6.5 %shard_map.105 = (f32[8,128]{1,0:T(8,128)}, f32[8,128]{1,0:T(8,128)}) custom-call(s32[1]{0:T(128)} %bitcast.123, f32[1024]{0:T(1024)} %get-tuple-element.25.prev_ref, f32[1024]{0:T(1024)} %get-tuple-element.24.before_ref, f32[512]{0:T(512)} %fusion.86.gain_ref, f32[8,128]{1,0:T(8,128)} %bitcast.114, f32[8,128]{1,0:T(8,128)} %bitcast.115, ...), custom_call_target="tpu_custom_call" | custom-call | tf_op jit(solution)/shard_map/pallas_call | solution.py:326
  176.1 6.2 %all-to-all-start.4 = ((f32[2,512,2]{2,0,1:T(2,128)}), f32[2,512,2]{2,0,1:T(2,128)S(1)}, u32[]{:S(2)}, u32[]{:S(2)}) async-start(f32[2,512,2]{2,0,1:T(2,128)} %copy.112), calls=%async_computation.4 | async-start | bytes 1048576 | tf_op jit(solution)/shard_map/all_to_all | solution.py:445
  182.3 19.7 %all-to-all-done.4 = f32[2,512,2]{2,0,1:T(2,128)S(1)} async-done(((f32[2,512,2]{2,0,1:T(2,128)}), f32[2,512,2]{2,0,1:T(2,128)S(1)}, u32[]{:S(2)}, u32[]{:S(2)}) %all-to-all-start.4) | async-done | bytes 8224 | tf_op jit(solution)/shard_map/all_to_all | solution.py:445
  204.1 5.2 %all_to_all.86 = f32[2,4,256]{2,0,1:T(2,128)S(1)} all-to-all(f32[2,4,256]{2,0,1:T(2,128)S(1)} %copy.115), channel_id=1, replica_groups=mesh['grp'=128,'cores'=2] {'cores'}, dimensions={1} | all-to-all | bytes 16384 | tf_op jit(solution)/shard_map/all_to_all | solution.py:444
  209.4 9.8 %fusion.6 = f32[2,1024]{1,0:T(2,128)S(1)} fusion(s32[512]{0:T(512)S(1)} %fusion.93, f32[2,512]{1,0:T(2,128)S(1)} %bitcast.118, f32[512]{0:T(512)S(1)} %compare_select_fusion.2), kind=kOutput, calls=%fused_computation.17 | convolution fusion | flops 19923968 | bytes 16384 | tf_op jit(solution)/shard_map/dot_general | solution.py:464
  219.2 9.8 %fusion.20 = f32[2,1024]{1,0:T(2,128)S(1)} fusion(f32[2,1024]{1,0:T(2,128)S(1)} %fusion.6, s32[512]{0:T(512)S(1)} %fusion.93, f32[2,512]{1,0:T(2,128)S(1)} %bitcast.119, f32[512]{0:T(512)S(1)} %compare_select_fusion.2), kind=kOutput, calls=%fused_computation.45 | convolution fusion | flops 19926016 | bytes 24576 | tf_op jit(solution)/shard_map/dot_general | solution.py:462
  229.7 17.3 %all_to_all.87 = f32[128,2,128]{2,1,0:T(2,128)S(1)} all-to-all(f32[128,2,128]{2,1,0:T(2,128)S(1)} %copy.120), channel_id=1, replica_groups=mesh['grp'=128,'cores'=2] {'grp'}, dimensions={0} | all-to-all | bytes 262144 | tf_op jit(solution)/shard_map/all_to_all | solution.py:471
  (135 shorter events, 30.4 us)
Async XLA Ops:
  1.4 9.9 %copy-start.8 = (s32[64,1]{0,1:T(1,128)S(1)}, s32[64,1]{0,1:T(1,128)}, u32[]{:S(2)}) copy-start(s32[64,1]{0,1:T(1,128)} %param.11) | copy-start | bytes 772
  1.4 10.1 %copy-start.9 = (s32[64]{0:T(128)S(1)}, s32[64]{0:T(128)}, u32[]{:S(2)}) copy-start(s32[64]{0:T(128)} %param.12) | copy-start | bytes 772
  1.4 26.6 %copy-start.7 = (s32[64,6]{0,1:T(8,128)S(1)}, s32[64,6]{0,1:T(8,128)}, u32[]{:S(2)}) copy-start(s32[64,6]{0,1:T(8,128)} %param.10) | copy-start | bytes 4612
  1.4 26.7 %copy-start.4 = (f32[3,8,8]{2,1,0:T(8,128)S(1)}, f32[3,8,8]{2,1,0:T(8,128)}, u32[]{:S(2)}) copy-start(f32[3,8,8]{2,1,0:T(8,128)} %param.8) | copy-start | bytes 2308
  1.4 30.2 %copy-start.10 = (s32[64]{0:T(128)S(1)}, s32[64]{0:T(128)}, u32[]{:S(2)}) copy-start(s32[64]{0:T(128)} %param.9) | copy-start | bytes 772
  4.5 30.7 %collective-permute-start = (f32[8,64,384]{2,1,0:T(8,128)}, f32[8,64,384]{2,1,0:T(8,128)S(1)}, u32[]{:S(2)}, u32[]{:S(2)}) collective-permute-start(f32[8,64,384]{2,1,0:T(8,128)} %shard_map.102.own_ref), channel_id=1, source_target_pairs={{0,1},{1,2},{2,3},{3,4},{4,5},{5,6},{6,7},{7,8},{8,9},{9,10},{10,1... | collective-permute-start | bytes 2359304 | tf_op jit(solution)/shard_map/ppermute | solution.py:27
  9.4 25.8 %collective-permute-start.1 = (f32[8,64,384]{2,1,0:T(8,128)}, f32[8,64,384]{2,1,0:T(8,128)S(1)}, u32[]{:S(2)}, u32[]{:S(2)}) collective-permute-start(f32[8,64,384]{2,1,0:T(8,128)} %shard_map.102.own_ref), channel_id=1, source_target_pairs={{1,0},{2,1},{3,2},{4,3},{5,4},{6,5},{7,6},{8,7},{9,8},{10,9},{11,1... | collective-permute-start | bytes 2359304 | tf_op jit(solution)/shard_map/ppermute | solution.py:27
  12.5 62.4 %all-to-all-start = ((f32[128,1,2]{2,1,0:T(1,128)}), f32[128,1,2]{2,1,0:T(1,128)S(1)}, u32[]{:S(2)}, u32[]{:S(2)}) async-start(f32[128,1,2]{2,1,0:T(1,128)} %bitcast.4), calls=%async_computation | async-start | bytes 131072 | tf_op jit(solution)/shard_map/all_to_all | solution.py:405
  35.2 0.9 copy-start
  35.2 1.2 copy-start.1
  45.4 14.5 %collective-permute-start.2 = (f32[8,64,384]{2,1,0:T(8,128)}, f32[8,64,384]{2,1,0:T(8,128)S(1)}, u32[]{:S(2)}, u32[]{:S(2)}) collective-permute-start(f32[8,64,384]{2,1,0:T(8,128)} %get-tuple-element.11.own_ref), channel_id=1, source_target_pairs={{0,1},{1,2},{2,3},{3,4},{4,5},{5,6},{6,7},{7,8},{8,9},{9,10},{10,1... | collective-permute-start | bytes 2359304 | tf_op jit(solution)/shard_map/ppermute | solution.py:27
  50.7 13.5 %collective-permute-start.3 = (f32[8,64,384]{2,1,0:T(8,128)}, f32[8,64,384]{2,1,0:T(8,128)S(1)}, u32[]{:S(2)}, u32[]{:S(2)}) collective-permute-start(f32[8,64,384]{2,1,0:T(8,128)} %get-tuple-element.11.own_ref), channel_id=1, source_target_pairs={{1,0},{2,1},{3,2},{4,3},{5,4},{6,5},{7,6},{8,7},{9,8},{10,9},{11,1... | collective-permute-start | bytes 2359304 | tf_op jit(solution)/shard_map/ppermute | solution.py:27
  59.9 4.3 %copy-start.2 = (f32[8,64,384]{2,1,0:T(8,128)}, f32[8,64,384]{2,1,0:T(8,128)S(1)}, u32[]{:S(2)}) copy-start(f32[8,64,384]{2,1,0:T(8,128)S(1)} %collective-permute-done.2.prev_ref) | copy-start | bytes 2359300
  64.2 0.9 copy-start.3
  74.9 27.5 %all-to-all-start.1 = ((f32[128,2,128]{2,1,0:T(2,128)}), f32[128,2,128]{2,1,0:T(2,128)S(1)}, u32[]{:S(2)}, u32[]{:S(2)}) async-start(f32[128,2,128]{2,1,0:T(2,128)} %bitcast.6), calls=%async_computation.1 | async-start | bytes 262144 | tf_op jit(solution)/shard_map/all_to_all | solution.py:404
  102.8 8.7 %copy-start.5 = (f32[2,1024]{1,0:T(2,128)}, f32[2,1024]{1,0:T(2,128)S(1)}, u32[]{:S(2)}) copy-start(f32[2,1024]{1,0:T(2,128)S(1)} %reshape.301) | copy-start | bytes 24580
  121.4 35.7 %all-to-all-start.2 = ((f32[2,2,512]{1,0,2:T(2,128)}), f32[2,2,512]{1,0,2:T(2,128)S(1)}, u32[]{:S(2)}, u32[]{:S(2)}) async-start(f32[2,2,512]{1,0,2:T(2,128)} %copy.103), calls=%async_computation.2 | async-start | bytes 1048576 | tf_op jit(solution)/shard_map/all_to_all | solution.py:426
  176.1 25.9 %all-to-all-start.4 = ((f32[2,512,2]{2,0,1:T(2,128)}), f32[2,512,2]{2,0,1:T(2,128)S(1)}, u32[]{:S(2)}, u32[]{:S(2)}) async-start(f32[2,512,2]{2,0,1:T(2,128)} %copy.112), calls=%async_computation.4 | async-start | bytes 1048576 | tf_op jit(solution)/shard_map/all_to_all | solution.py:445
  229.0 18.9 %copy-start.6 = (f32[2,1024]{1,0:T(2,128)}, f32[2,1024]{1,0:T(2,128)S(1)}, u32[]{:S(2)}) copy-start(f32[2,1024]{1,0:T(2,128)S(1)} %fusion.20) | copy-start | bytes 24580

commit v2 on v1

--- a/solution.py
+++ b/solution.py
@@ -3,6 +3,7 @@
 
 import jax
 import jax.numpy as jnp
+import numpy as np
 from jax import lax
 from jax.experimental import pallas as pl
 from jax.experimental.pallas import tpu as pltpu
@@ -56,6 +57,29 @@
 def split_two(value):
     high = value.astype(jnp.bfloat16)
     return high, (value - high.astype(jnp.float32)).astype(jnp.bfloat16)
+
+
+def split_three(value):
+    high = value.astype(jnp.bfloat16)
+    return (high,) + split_two(value - high.astype(jnp.float32))
+
+
+def sum_of_parts(parts):
+    return parts[0] + (parts[1] + parts[2])
+
+
+def product_of_parts(parts, right):
+    return [product(part, right) for part in parts]
+
+
+def exact(left, right, left_dim=1, right_dim=0):
+    return lax.dot_general(
+        left,
+        right,
+        (((left_dim,), (right_dim,)), ((), ())),
+        precision=HIGHEST_PRECISION,
+        preferred_element_type=jnp.float32,
+    )
 
 
 def product(left, right):
@@ -89,6 +113,8 @@
     expand_ref,
     rate_ref,
     select_ref,
+    place_ref,
+    segment_ref,
     out_ref,
     extra_ref,
     ghost_ref,
@@ -175,12 +201,15 @@
         total = flow_ref[0] * out_ref[0]
         for v in range(1, variables):
             total = total + flow_ref[v] * out_ref[v]
-        high, rest = total.astype(jnp.bfloat16), None
-        rest = total - high.astype(jnp.float32)
-        middle, low = split_two(rest)
-        selection = select_ref[...]
-        extra_ref[...] = product(high, selection) + (
-            product(middle, selection) + product(low, selection)
+        patches = sum_of_parts(product_of_parts(split_three(total), select_ref[...]))
+        parts = jnp.concatenate(split_three(patches) + (segment_ref[...],), axis=1)
+        sent = [product(place_ref[0], parts), product(place_ref[1], parts)]
+        for k in range(2):
+            extra_ref[:, 128 * k : 128 * k + 128] = sum_of_parts(
+                [sent[k][:, 128 * i : 128 * i + 128] for i in range(3)]
+            )
+        extra_ref[:, 256:384] = jnp.where(
+            iota((128, 128), 1) < 64, sent[0][:, 384:512], sent[1][:, 384:512]
         )
     else:
         write_faces(out_ref, select_ref, extra_ref)
@@ -201,16 +230,16 @@
     )(state_in, selection)
 
 
-def advance(mix, speeds, flow, state_in, prev, own, following, pick, expand, rate, selection, last):
+def advance(mix, speeds, flow, state_in, prev, own, following, pick, expand, rate, selection, place, segment, last):
     variables, blocks = state_in.shape[:2]
-    extra = (blocks, 128) if last else (variables, blocks, 384)
+    extra = (128, 384) if last else (variables, blocks, 384)
     return pl.pallas_call(
         functools.partial(step_kernel, last=last),
         out_shape=(
             jax.ShapeDtypeStruct(state_in.shape, jnp.float32),
             jax.ShapeDtypeStruct(extra, jnp.float32),
         ),
-        in_specs=[SMEM_SPEC] * 3 + [VMEM_SPEC] * 8,
+        in_specs=[SMEM_SPEC] * 3 + [VMEM_SPEC] * 10,
         out_specs=(VMEM_SPEC, VMEM_SPEC),
         scratch_shapes=[
             pltpu.VMEM((2, 64 * variables, 256), jnp.bfloat16),
@@ -218,7 +247,7 @@
             pltpu.VMEM((variables, 64, 128), jnp.float32),
         ],
         interpret=INTERPRET,
-    )(mix, speeds, flow, state_in, prev, own, following, pick, expand, rate, selection)
+    )(mix, speeds, flow, state_in, prev, own, following, pick, expand, rate, selection, place, segment)
 
 
 def block_picks(neighbours, offset):
@@ -234,11 +263,108 @@
     return jnp.max(jnp.sum(jnp.abs(flux_derivative_matrices), axis=2), axis=1)
 
 
-def fourier_tables(orders):
-    longitudes = jnp.arange(NLON, dtype=jnp.int32)
-    phase_index = longitudes[:, None] * orders[None, :] % NLON
-    angle_rad = phase_index.astype(jnp.float32) * (2.0 * math.pi / NLON)
-    return (jnp.cos(angle_rad), jnp.sin(angle_rad))
+def transform_tables():
+    column = np.arange(64)
+    q, imaginary = 2 * (column // 8) + column % 2, column // 4 % 2 == 1
+    s, r, n = np.arange(16), np.arange(64), np.arange(32)
+    step = 2.0 * np.pi * np.outer(s, q) / 16
+    twist = 2.0 * np.pi * np.outer(r, q) / NLON
+    wave = 2.0 * np.pi * np.outer(n, r) / 64
+    split = np.concatenate([np.cos(step), -np.sin(step)], axis=1)
+    twiddle = np.stack([np.cos(twist), np.sin(twist)])
+    forward = np.concatenate([np.cos(wave), np.sin(wave)], axis=1) / NLON
+    backward = np.concatenate([np.cos(wave), np.sin(wave)], axis=0).T
+    factor = np.where((n[:, None] == 0) & (q[None, :] == 0), 1.0, 2.0)
+    untwist = np.stack(
+        [
+            np.where(imaginary, -np.sin(twist), np.cos(twist)),
+            np.where(imaginary, -np.cos(twist), -np.sin(twist)),
+        ]
+    )
+    of_latitude = [(column // 2 % 2 == latitude)[None, :] for latitude in range(2)]
+    join = np.concatenate(
+        [np.concatenate([np.cos(step) * own, np.sin(step) * own], axis=1) for own in of_latitude]
+    )
+    return [
+        jnp.asarray(table.astype(np.float32))
+        for table in (split, twiddle, forward, factor, backward, untwist, join)
+    ]
+
+
+def landing_of(codes, k):
+    return codes[:, 64 * k : 64 * k + 16] == (iota((128, 16), 1) + 1).astype(jnp.float32)
+
+
+def forward_kernel(got_ref, split_ref, twiddle_ref, forward_ref, grid_ref, send_ref):
+    grid = None
+    codes = got_ref[:, 256:384]
+    for k in range(2):
+        landing = landing_of(codes, k).astype(jnp.float32)
+        part = exact(landing, got_ref[:, 128 * k : 128 * k + 128], 0, 0)
+        grid = part if grid is None else grid + part
+    grid_ref[...] = grid
+    column = iota((64, 64), 1)
+    split = split_ref[...]
+    first, second = exact(grid[:, 0:64], split, 0, 0), exact(grid[:, 64:128], split, 0, 0)
+    of_first = column // 2 % 2 == 0
+    even = jnp.where(of_first, first[:, 0:64], second[:, 0:64])
+    odd = jnp.where(of_first, first[:, 64:128], second[:, 64:128])
+    turned_re = even * twiddle_ref[0] + odd * twiddle_ref[1]
+    turned_im = odd * twiddle_ref[0] - even * twiddle_ref[1]
+    real = column // 4 % 2 == 0
+    both = jnp.concatenate(
+        [jnp.where(real, turned_re, turned_im), jnp.where(real, turned_im, -turned_re)], axis=0
+    )
+    coef = exact(forward_ref[...], both)
+    for part in range(8):
+        send_ref[32 * part : 32 * part + 32, :] = coef[:, 8 * part : 8 * part + 8]
+
+
+def backward_kernel(
+    synth_ref, got_ref, factor_ref, backward_ref, untwist_ref, join_ref, grid_ref, back_ref, pair_ref
+):
+    for part in range(8):
+        columns = slice(8 * part, 8 * part + 8)
+        values = synth_ref[32 * part : 32 * part + 32, :]
+        pair_ref[0:32, columns] = values
+        pair_ref[32:64, columns] = jnp.concatenate([-values[:, 4:8], values[:, 0:4]], axis=1)
+    factor = factor_ref[...]
+    pair = pair_ref[...] * jnp.concatenate([factor, factor], axis=0)
+    rows = exact(backward_ref[...], pair)
+    turned = jnp.concatenate([rows * untwist_ref[0], rows * untwist_ref[1]], axis=1)
+    joined = exact(join_ref[...], turned, 1, 1)
+    grid_ref[:, 0:64] = joined[0:16]
+    grid_ref[:, 64:128] = joined[16:32]
+    parts = jnp.concatenate(split_three(grid_ref[...]), axis=1)
+    codes = got_ref[:, 256:384]
+    for k in range(2):
+        found = product(landing_of(codes, k).astype(jnp.float32).astype(jnp.bfloat16), parts)
+        back_ref[:, 128 * k : 128 * k + 128] = sum_of_parts(
+            [found[:, 128 * i : 128 * i + 128] for i in range(3)]
+        )
+
+
+def home_kernel(home_ref, place_ref, shell_ref):
+    total = None
+    for k in range(2):
+        parts = jnp.concatenate(split_three(home_ref[:, 128 * k : 128 * k + 128]), axis=1)
+        found = lax.dot_general(
+            place_ref[k], parts, (((0,), (0,)), ((), ())), preferred_element_type=jnp.float32
+        )
+        part = sum_of_parts([found[:, 128 * i : 128 * i + 128] for i in range(3)])
+        total = part if total is None else total + part
+    shell_ref[...] = total
+
+
+def run_kernel(kernel, operands, shapes, scratch=()):
+    return pl.pallas_call(
+        kernel,
+        out_shape=tuple(jax.ShapeDtypeStruct(shape, jnp.float32) for shape in shapes),
+        in_specs=[VMEM_SPEC] * len(operands),
+        out_specs=tuple([VMEM_SPEC] * len(shapes)),
+        scratch_shapes=[pltpu.VMEM(shape, jnp.float32) for shape in scratch],
+        interpret=INTERPRET,
+    )(*operands)
 
 
 def legendre_start(sine_lat, orders):
@@ -250,10 +376,7 @@
         ]
     )
     log_base = jnp.take(log_sums, orders)
-    order_real = orders.astype(jnp.float32)
-    return jnp.exp(
-        0.5 * math.log(0.5) + log_base[None, :] + order_real[None, :] * jnp.log(sine_lat)[:, None]
-    )
+    return jnp.exp(0.5 * math.log(0.5) + log_base + orders.astype(jnp.float32) * jnp.log(sine_lat))
 
 
 def recurrence_factors(orders):
@@ -311,14 +434,15 @@
     out_im[...] = carried[3]
 
 
-def solve_spectral(coef_re, coef_im, cosine_lat, sine_lat, weights_lat, orders):
-    def folded(rows):
-        return jnp.swapaxes(rows.reshape(2, 4, 128), 0, 1).reshape(8, 128)
-
-    def unfolded(value):
-        return jnp.swapaxes(value.reshape(4, 2, 128), 0, 1).reshape(2, 512)
-
-    diagonal = folded(jnp.transpose(legendre_start(sine_lat, orders)))
+def solve_spectral(received, first_order, lat_total):
+    rows = received.reshape(2, 128, 2, 4).transpose(2, 0, 3, 1).reshape(2, 8, 128)
+    row, lane = iota((8, 128), 0), iota((8, 128), 1)
+    lat_ids = 256 * (row // 4) + 2 * lane + row // 2 % 2
+    colatitude = (lat_ids.astype(jnp.float32) + 0.5) * (math.pi / lat_total)
+    cosine, sine = jnp.cos(colatitude), jnp.sin(colatitude)
+    weights = math.pi / lat_total * sine
+    orders = first_order + jnp.arange(2, dtype=jnp.int32)
+    diagonal = legendre_start(sine, jnp.broadcast_to(jnp.tile(orders, 4)[:, None], (8, 128)))
     coef_prev, coef_before = recurrence_factors(orders)
     degree_real = jnp.arange(DEGREES, dtype=jnp.int32).astype(jnp.float32)
     gain = POT_GAIN / (degree_real * (degree_real + 1.0) + KAPPA2)
@@ -334,12 +458,13 @@
         coef_prev.reshape(-1),
         coef_before.reshape(-1),
         gain,
-        folded(coef_re * weights_lat[None, :]),
-        folded(coef_im * weights_lat[None, :]),
+        rows[0] * weights,
+        rows[1] * weights,
         diagonal,
-        folded(jnp.broadcast_to(cosine_lat[None, :], (2, 512))),
-    )
-    return unfolded(acc_re), unfolded(acc_im)
+        cosine,
+    )
+    both = jnp.stack([acc_re, acc_im]).reshape(2, 2, 4, 128)
+    return both.transpose(1, 3, 0, 2).reshape(256, 8)
 
 
 def body(
@@ -365,6 +490,19 @@
     rate = jnp.broadcast_to(rate_block[:, None], (block_portion, 128))
     mix = 0.5 * flux_derivative_matrices.reshape(-1)
     half_speeds = 0.5 * speeds
+    band_index = block_latitude_band[:, 0]
+    block_ids = jnp.arange(block_portion, dtype=jnp.int32)
+    earlier = (band_index[None, :] == band_index[:, None]) & (
+        block_ids[None, :] < block_ids[:, None]
+    )
+    rank_in_band = jnp.sum(earlier.astype(jnp.int32), axis=1)
+    shape = (2, grp_size, block_portion)
+    place = (
+        (band_index[None, None, :] == iota(shape, 1)) & (rank_in_band[None, None, :] == iota(shape, 0))
+    ).astype(jnp.bfloat16)
+    segment = jnp.broadcast_to(
+        (block_longitude_segment + 1).astype(jnp.bfloat16)[:, None], (block_portion, 128)
+    )
     parallel_flow_charge = invariant_fluid_quantities
     faces = make_faces(parallel_flow_charge, selection)
     for section_index in range(STEPS):
@@ -381,95 +519,31 @@
             expand,
             rate,
             patch_selection() if last else selection,
+            place,
+            segment,
             last,
         )
-    patches = faces
-    band_index = block_latitude_band[:, 0]
-    block_ids = jnp.arange(block_portion, dtype=jnp.int32)
-    earlier = (band_index[None, :] == band_index[:, None]) & (
-        block_ids[None, :] < block_ids[:, None]
-    )
-    rank_in_band = jnp.sum(earlier.astype(jnp.int32), axis=1)
-    capacity = max(2, 2 * block_portion // grp_size)
-    slot_index = band_index * capacity + rank_in_band
-    slot_ids = jnp.arange(grp_size * capacity, dtype=jnp.int32)
-    placing = (slot_ids[:, None] == slot_index[None, :]).astype(jnp.float32)
-    send_rows = jnp.dot(placing, patches, precision=HIGHEST_PRECISION).reshape(
-        grp_size, capacity, 128
-    )
-    send_codes = jnp.dot(
-        placing, (block_longitude_segment + 1).astype(jnp.float32), precision=HIGHEST_PRECISION
-    ).reshape(grp_size, capacity)
-    got_rows, got_codes = (
-        lax.all_to_all(send_rows, "grp", split_axis=0, concat_axis=0, tiled=True),
-        lax.all_to_all(send_codes, "grp", split_axis=0, concat_axis=0, tiled=True),
-    )
-    segments = NLON // 64
-    segment_codes = jnp.arange(1, segments + 1, dtype=jnp.int32).astype(jnp.float32)
-    landing = (got_codes.reshape(-1)[:, None] == segment_codes[None, :]).astype(jnp.float32)
-    gathered = jnp.dot(landing.T, got_rows.reshape(-1, 128), precision=HIGHEST_PRECISION)
-    fac_local = jnp.swapaxes(gathered.reshape(segments, LAT_DEV, 64), 0, 1).reshape(LAT_DEV, NLON)
-    orders_all = jnp.arange(DEGREES, dtype=jnp.int32)
-    cos_table, sin_table = fourier_tables(orders_all)
-    coef_re = jnp.dot(fac_local, cos_table, precision=HIGHEST_PRECISION) / NLON
-    coef_im = -jnp.dot(fac_local, sin_table, precision=HIGHEST_PRECISION) / NLON
-    lat_total = LAT_DEV * device_total
-    degree_share = DEGREES // device_total
-    lat_ids = jnp.arange(lat_total, dtype=jnp.int32)
-    colatitude = (lat_ids.astype(jnp.float32) + 0.5) * (math.pi / lat_total)
-    cosine_all = jnp.cos(colatitude)
-    sine_all = jnp.sin(colatitude)
-    weights_all = math.pi / lat_total * sine_all
-    own_orders = device * degree_share + jnp.arange(degree_share, dtype=jnp.int32)
-    stacked = jnp.stack([coef_re, coef_im])
-    regrouped = lax.all_to_all(
-        lax.all_to_all(stacked, "grp", split_axis=2, concat_axis=1, tiled=True),
-        "cores",
-        split_axis=2,
-        concat_axis=1,
-        tiled=True,
-    )
-    regrouped = jnp.transpose(
-        regrouped.reshape(2, core_size, grp_size, LAT_DEV, degree_share), (0, 2, 1, 3, 4)
-    ).reshape(2, lat_total, degree_share)
-    synth_re, synth_im = solve_spectral(
-        jnp.transpose(regrouped[0]),
-        jnp.transpose(regrouped[1]),
-        cosine_all,
-        sine_all,
-        weights_all,
-        own_orders,
-    )
-    synth_both = jnp.stack([jnp.transpose(synth_re), jnp.transpose(synth_im)])
-    returned = lax.all_to_all(
-        lax.all_to_all(synth_both, "grp", split_axis=1, concat_axis=2, tiled=True),
-        "cores",
-        split_axis=1,
-        concat_axis=2,
-        tiled=True,
-    )
-    column_ids = jnp.arange(DEGREES, dtype=jnp.int32)
-    order_perm = (
-        degree_share
-        * (
-            core_size * (column_ids // degree_share % grp_size)
-            + column_ids // (grp_size * degree_share)
-        )
-        + column_ids % degree_share
-    )
-    cos_perm, sin_perm = fourier_tables(order_perm)
-    factor = jnp.where(order_perm == 0, jnp.float32(1.0), jnp.float32(2.0))
-    potential_local = jnp.dot(
-        returned[0] * factor, cos_perm.T, precision=HIGHEST_PRECISION
-    ) - jnp.dot(returned[1] * factor, sin_perm.T, precision=HIGHEST_PRECISION)
-    grid_segments = jnp.swapaxes(potential_local.reshape(LAT_DEV, segments, 64), 0, 1).reshape(
-        segments, 128
-    )
-    back_rows = jnp.dot(landing, grid_segments, precision=HIGHEST_PRECISION).reshape(
-        grp_size, capacity, 128
-    )
-    home_rows = lax.all_to_all(back_rows, "grp", split_axis=0, concat_axis=0, tiled=True)
-    shell_potential = jnp.dot(placing.T, home_rows.reshape(-1, 128), precision=HIGHEST_PRECISION)
+    split, twiddle, forward, factor, backward, untwist, join = transform_tables()
+    got = lax.all_to_all(faces, "grp", split_axis=0, concat_axis=0, tiled=True)
+    fac_segments, coef = run_kernel(
+        forward_kernel, (got, split, twiddle, forward), ((16, 128), (device_total, 8))
+    )
+    axes = ("grp", "cores")
+    received = lax.all_to_all(coef, axes, split_axis=0, concat_axis=0, tiled=True)
+    synth = solve_spectral(received, 16 * (device % 32) + 2 * (device // 32), LAT_DEV * device_total)
+    returned = lax.all_to_all(synth, axes, split_axis=0, concat_axis=0, tiled=True)
+    grid_segments, back = run_kernel(
+        backward_kernel,
+        (returned, got, factor, backward, untwist, join),
+        ((16, 128), (grp_size, 256)),
+        scratch=((64, 64),),
+    )
+    home = lax.all_to_all(back, "grp", split_axis=0, concat_axis=0, tiled=True)
+    (shell_potential,) = run_kernel(home_kernel, (home, place), ((block_portion, 128),))
+    fac_local, potential_local = (
+        jnp.swapaxes(grid.reshape(16, LAT_DEV, 64), 0, 1).reshape(LAT_DEV, NLON)
+        for grid in (fac_segments, grid_segments)
+    )
     return (parallel_flow_charge, fac_local, potential_local, shell_potential)
 
 

time: 252 us -> 168 us (0.67); the launches traced: 248 us -> 167 us
  matrix products: 40.3 us -> 0 us
  starting transfers between devices: 65.8 us -> 42.8 us
  waiting for transfers between devices: 58.8 us -> 37.4 us
  Pallas kernels: 26.8 us -> 34.2 us
  blocking collectives: 27.8 us -> 21.1 us
  local copies, waits for them, and re-layouts: 16.7 us -> 20.7 us
    dot_general x9 -> x0, matrix products: 40.3 us -> none  [the longest x1 9.83 us: body(): jnp.dot(returned[1] * factor, sin_perm.T, precision=HIGHEST_PRECISION)]
    all_to_all x4 -> x3, waiting for transfers between devices: 48.5 us -> 24.7 us  [the longest x1 9.92 us: body(): got = lax.all_to_all(faces, 'grp', split_axis=0, concat_axis=0, tiled=True)]
    all_to_all x4 -> x3, starting transfers between devices: 51.8 us -> 31.6 us  [the longest x1 20 us: body(): got = lax.all_to_all(faces, 'grp', split_axis=0, concat_axis=0, tiled=True)]
    pallas_call x0 -> x3, Pallas kernels: none -> 7.2 us  [run_kernel(): pl.pallas_call(kernel, out_shape=tuple((jax.ShapeDtypeStruct(shape, jnp.f...]
    all_to_all x3 -> x1, blocking collectives: 27.8 us -> 21.1 us  [body(): lax.all_to_all(synth, axes, split_axis=0, concat_axis=0, tiled=True)]
    gather x1, local copies, waits for them, and re-layouts: 0.64 us -> 6.87 us  [legendre_start(): log_base = jnp.take(log_sums, orders)]
    unnamed x24 -> x28, local copies, waits for them, and re-layouts: 1.27 us -> 4.96 us
    ppermute x4, starting transfers between devices: 14 us -> 11.2 us  [passed_along(): lax.ppermute(value, axis, [(source, source + steps) for source in range(l...]
  transfers between devices with their start and end apart: 8 -> 7, of which waited for: 5 -> 6; matrix products, arithmetic and copies ran while one was open for 6% -> 11% of each run, Pallas kernels for 7% -> 0%
where the time goes in v2:
time: 168 us; the launch traced here: 167 us
  starting transfers between devices  42.8 us (25%)
  waiting for transfers between devices  37.4 us (22%)
  Pallas kernels  34.2 us (20%)
  blocking collectives  21.1 us (13%)
  local copies, waits for them, and re-layouts  20.7 us (12%)
  other arithmetic  9.92 us (6%)
    all_to_all x1, blocking collectives, body(): lax.all_to_all(synth, axes, split_axis=0, concat_axis=0, tiled=True)  21.1 us
    all_to_all x1, starting transfers between devices, body(): got = lax.all_to_all(faces, 'grp', split_axis=0, concat_axis=0, tiled=True)  20 us
    pallas_call x2, Pallas kernels, advance(): pl.pallas_call(functools.partial(step_kernel, last=last), out_shape=(jax....  17.4 us
    ppermute x4, waiting for transfers between devices, passed_along(): lax.ppermute(value, axis, [(source, source + steps) for source in range(l...  12.7 us
    ppermute x4, starting transfers between devices, passed_along(): lax.ppermute(value, axis, [(source, source + steps) for source in range(l...  11.2 us
    all_to_all x1, waiting for transfers between devices, body(): got = lax.all_to_all(faces, 'grp', split_axis=0, concat_axis=0, tiled=True)  9.92 us
    all_to_all x1, waiting for transfers between devices, body(): home = lax.all_to_all(back, 'grp', split_axis=0, concat_axis=0, tiled=True)  9.8 us
    pallas_call x3, Pallas kernels, run_kernel(): pl.pallas_call(kernel, out_shape=tuple((jax.ShapeDtypeStruct(shape, jnp.f...  7.2 us
  transfers between devices with their start and end apart: 7, of which 6 were waited for; matrix products, arithmetic and copies ran while one was open for 11% of the time, Pallas kernels for 0%

profile of v2, /device:TPU:1, one launch (start us, length us, event | category | flops | bytes accessed | tf_op | source)
XLA Modules:
  0.0 167.0 jit_solution(8699375977078621204)
XLA Ops:
  1.5 3.0 %shard_map.165.own_ref = f32[8,64,384]{2,1,0:T(8,128)} custom-call(f32[8,64,512]{2,1,0:T(8,128)} %state_ref.3, bf16[512,256]{1,0:T(8,128)(2,1)} %fusion.15.select_ref), custom_call_target="tpu_custom_call" | custom-call | tf_op jit(solution)/shard_map/pallas_call | solution.py:224
  4.4 4.9 %collective-permute-start = (f32[8,64,384]{2,1,0:T(8,128)}, f32[8,64,384]{2,1,0:T(8,128)S(1)}, u32[]{:S(2)}, u32[]{:S(2)}) collective-permute-start(f32[8,64,384]{2,1,0:T(8,128)} %shard_map.165.own_ref), channel_id=1, source_target_pairs={{0,1},{1,2},{2,3},{3,4},{4,5},{5,6},{6,7},{7,8},{8,9},{9,10},{10,1... | collective-permute-start | bytes 2359304 | tf_op jit(solution)/shard_map/ppermute | solution.py:28
  9.4 1.9 %collective-permute-start.1 = (f32[8,64,384]{2,1,0:T(8,128)}, f32[8,64,384]{2,1,0:T(8,128)S(1)}, u32[]{:S(2)}, u32[]{:S(2)}) collective-permute-start(f32[8,64,384]{2,1,0:T(8,128)} %shard_map.165.own_ref), channel_id=1, source_target_pairs={{1,0},{2,1},{3,2},{4,3},{5,4},{6,5},{7,6},{8,7},{9,8},{10,9},{11,1... | collective-permute-start | bytes 2359304 | tf_op jit(solution)/shard_map/ppermute | solution.py:28
  20.7 2.2 %collective-permute-done.1.next_ref = f32[8,64,384]{2,1,0:T(8,128)S(1)} collective-permute-done((f32[8,64,384]{2,1,0:T(8,128)}, f32[8,64,384]{2,1,0:T(8,128)S(1)}, u32[]{:S(2)}, u32[]{:S(2)}) %collective-permute-start.1) | collective-permute-done | bytes 786464 | tf_op jit(solution)/shard_map/ppermute | solution.py:28
  24.4 9.0 %shard_map.166 = (f32[8,64,512]{2,1,0:T(8,128)}, f32[8,64,384]{2,1,0:T(8,128)}) custom-call(f32[192]{0:T(256)} %mul.173.mix_ref, f32[3]{0:T(128)} %broadcast_multiply_fusion.1.speed_ref, f32[8]{0:T(128)} %flow_ref.3, f32[8,64,512]{2,1,0:T(8,128)} %state_ref.3, f32[8,64,384]{2,1,0:T(8,128)} %copy-done, f32[8,64,384]{2,1,0:T(8,128)} %shard_map.165.own_ref, ...), custom_call_target="tpu_custom_call" | custom-call | tf_op jit(solution)/shard_map/pallas_call | solution.py:236
  33.4 1.9 %collective-permute-start.2 = (f32[8,64,384]{2,1,0:T(8,128)}, f32[8,64,384]{2,1,0:T(8,128)S(1)}, u32[]{:S(2)}, u32[]{:S(2)}) collective-permute-start(f32[8,64,384]{2,1,0:T(8,128)} %get-tuple-element.15.own_ref), channel_id=1, source_target_pairs={{0,1},{1,2},{2,3},{3,4},{4,5},{5,6},{6,7},{7,8},{8,9},{9,10},{10,1... | collective-permute-start | bytes 2359304 | tf_op jit(solution)/shard_map/ppermute | solution.py:28
  35.3 2.5 %collective-permute-start.3 = (f32[8,64,384]{2,1,0:T(8,128)}, f32[8,64,384]{2,1,0:T(8,128)S(1)}, u32[]{:S(2)}, u32[]{:S(2)}) collective-permute-start(f32[8,64,384]{2,1,0:T(8,128)} %get-tuple-element.15.own_ref), channel_id=1, source_target_pairs={{1,0},{2,1},{3,2},{4,3},{5,4},{6,5},{7,6},{8,7},{9,8},{10,9},{11,1... | collective-permute-start | bytes 2359304 | tf_op jit(solution)/shard_map/ppermute | solution.py:28
  38.6 5.9 %collective-permute-done.2.prev_ref = f32[8,64,384]{2,1,0:T(8,128)S(1)} collective-permute-done((f32[8,64,384]{2,1,0:T(8,128)}, f32[8,64,384]{2,1,0:T(8,128)S(1)}, u32[]{:S(2)}, u32[]{:S(2)}) %collective-permute-start.2) | collective-permute-done | bytes 786464 | tf_op jit(solution)/shard_map/ppermute | solution.py:28
  44.5 4.6 %collective-permute-done.3.next_ref = f32[8,64,384]{2,1,0:T(8,128)S(1)} collective-permute-done((f32[8,64,384]{2,1,0:T(8,128)}, f32[8,64,384]{2,1,0:T(8,128)S(1)}, u32[]{:S(2)}, u32[]{:S(2)}) %collective-permute-start.3) | collective-permute-done | bytes 786464 | tf_op jit(solution)/shard_map/ppermute | solution.py:28
  50.0 8.4 %shard_map.167 = (f32[8,64,512]{2,1,0:T(8,128)}, f32[128,384]{1,0:T(8,128)}) custom-call(f32[192]{0:T(256)} %mul.173.mix_ref, f32[3]{0:T(128)} %broadcast_multiply_fusion.1.speed_ref, f32[8]{0:T(128)} %flow_ref.3, f32[8,64,512]{2,1,0:T(8,128)} %get-tuple-element.14.state_ref, f32[8,64,384]{2,1,0:T(8,128)} %copy-done.2, ...), custom_call_target="tpu_custom_call" | custom-call | tf_op jit(solution)/shard_map/pallas_call | solution.py:236
  58.4 1.8 %copy.47 = f32[128,1,384]{2,1,0:T(1,128)} copy(f32[128,1,384]{2,0,1:T(8,128)} %bitcast.51) | data formatting | bytes 393216 | tf_op jit(solution)/shard_map/all_to_all | solution.py:527
  60.2 20.0 %all-to-all-start = ((f32[128,1,384]{2,1,0:T(1,128)}), f32[128,1,384]{2,1,0:T(1,128)S(1)}, u32[]{:S(2)}, u32[]{:S(2)}) async-start(f32[128,1,384]{2,1,0:T(1,128)} %copy.47), calls=%async_computation | async-start | bytes 393216 | tf_op jit(solution)/shard_map/all_to_all | solution.py:527
  82.1 9.9 %all-to-all-done = f32[128,1,384]{2,1,0:T(1,128)S(1)} async-done(((f32[128,1,384]{2,1,0:T(1,128)}), f32[128,1,384]{2,1,0:T(1,128)S(1)}, u32[]{:S(2)}, u32[]{:S(2)}) %all-to-all-start) | async-done | bytes 196640 | tf_op jit(solution)/shard_map/all_to_all | solution.py:527
  92.7 2.8 %shard_map.168 = (f32[16,128]{1,0:T(8,128)}, f32[256,8]{1,0:T(8,128)}) custom-call(f32[128,384]{1,0:T(8,128)} %bitcast.47, f32[16,128]{1,0:T(8,128)} %constant.295.clone.split_ref, f32[2,64,64]{2,1,0:T(8,128)} %constant.296.clone.twiddle_ref, f32[32,128]{1,0:T(8,128)} %constant.297.clone.forward_ref), custom_call_target="tpu_custom_call" | custom-call | tf_op jit(solution)/shard_map/pallas_call | solution.py:360
  95.5 5.3 %all-to-all-start.1 = ((f32[256,1,8]{2,1,0:T(1,128)}), f32[256,1,8]{2,1,0:T(1,128)S(1)}, u32[]{:S(2)}, u32[]{:S(2)}) async-start(f32[256,1,8]{2,1,0:T(1,128)} %bitcast.52), calls=%async_computation.1 | async-start | bytes 262144 | tf_op jit(solution)/shard_map/all_to_all | solution.py:532
  100.9 6.9 %gather_fusion = f32[1024]{0:T(1024)S(1)} fusion(f32[512]{0:T(512)S(1)} %pad_maximum_fusion.1, s32[1024]{0:T(1024)S(1)} %bitcast_clamp_fusion), kind=kCustom, calls=%fused_computation | custom fusion | bytes 12288 | tf_op jit(solution)/shard_map/jit(_take)/gather | solution.py:378
  107.8 5.0 %all-to-all-done.1 = f32[256,1,8]{2,1,0:T(1,128)S(1)} async-done(((f32[256,1,8]{2,1,0:T(1,128)}), f32[256,1,8]{2,1,0:T(1,128)S(1)}, u32[]{:S(2)}, u32[]{:S(2)}) %all-to-all-start.1) | async-done | bytes 8224 | tf_op jit(solution)/shard_map/all_to_all | solution.py:532
  113.5 6.6 %shard_map.169 = (f32[8,128]{1,0:T(8,128)}, f32[8,128]{1,0:T(8,128)}) custom-call(s32[1]{0:T(128)} %bitcast.63, f32[1024]{0:T(1024)} %get-tuple-element.31.prev_ref, f32[1024]{0:T(1024)} %get-tuple-element.30.before_ref, f32[512]{0:T(512)} %fusion.35.gain_ref, f32[8,128]{1,0:T(8,128)} %get-tuple-element.34.re_ref, f32[8,128]{1,0:T(8,128)} %get-tuple-element.33.im_ref, ...), custom_call_target="tpu_custom_call" | custom-call | tf_op jit(solution)/shard_map/pallas_call | solution.py:450
  121.6 21.1 %all_to_all.42 = f32[256,1,8]{2,1,0:T(1,128)} all-to-all(f32[256,1,8]{2,1,0:T(1,128)S(1)} %copy.55), channel_id=1, replica_groups=mesh['grp'=128,'cores'=2] {'grp','cores'}, dimensions={0} | all-to-all | bytes 16384 | tf_op jit(solution)/shard_map/all_to_all | solution.py:534
  142.7 2.6 %shard_map.170 = (f32[16,128]{1,0:T(8,128)}, f32[128,256]{1,0:T(8,128)}) custom-call(f32[256,8]{1,0:T(8,128)} %bitcast.49, f32[128,384]{1,0:T(8,128)} %bitcast.48, f32[32,64]{1,0:T(8,128)} %constant.298.clone.factor_ref, f32[64,64]{1,0:T(8,128)} %constant.299.clone.backward_ref, f32[2,64,64]{2,1,0:T(8,128)} %constant.300.clone.untwist_ref, ...), custom_call_target="tpu_custom_call" | custom-call | tf_op jit(solution)/shard_map/pallas_call | solution.py:360
  145.3 1.7 %copy.57 = f32[128,1,256]{2,1,0:T(1,128)} copy(f32[128,1,256]{2,0,1:T(8,128)} %bitcast.53) | data formatting | bytes 262144 | tf_op jit(solution)/shard_map/all_to_all | solution.py:541
  147.0 6.3 %all-to-all-start.3 = ((f32[128,1,256]{2,1,0:T(1,128)}), f32[128,1,256]{2,1,0:T(1,128)S(1)}, u32[]{:S(2)}, u32[]{:S(2)}) async-start(f32[128,1,256]{2,1,0:T(1,128)} %copy.57), calls=%async_computation.3 | async-start | bytes 262144 | tf_op jit(solution)/shard_map/all_to_all | solution.py:541
  154.8 9.8 %all-to-all-done.3 = f32[128,1,256]{2,1,0:T(1,128)S(1)} async-done(((f32[128,1,256]{2,1,0:T(1,128)}), f32[128,1,256]{2,1,0:T(1,128)S(1)}, u32[]{:S(2)}, u32[]{:S(2)}) %all-to-all-start.3) | async-done | bytes 131104 | tf_op jit(solution)/shard_map/all_to_all | solution.py:541
  165.3 1.7 %shard_map.171 = f32[64,128]{1,0:T(8,128)} custom-call(f32[128,256]{1,0:T(8,128)} %bitcast.50, bf16[2,128,64]{2,1,0:T(8,128)(2,1)} %fusion.19.place_ref), custom_call_target="tpu_custom_call" | custom-call | tf_op jit(solution)/shard_map/pallas_call | solution.py:360
  (101 shorter events, 20.3 us)
Async XLA Ops:
  4.4 16.3 %collective-permute-start = (f32[8,64,384]{2,1,0:T(8,128)}, f32[8,64,384]{2,1,0:T(8,128)S(1)}, u32[]{:S(2)}, u32[]{:S(2)}) collective-permute-start(f32[8,64,384]{2,1,0:T(8,128)} %shard_map.165.own_ref), channel_id=1, source_target_pairs={{0,1},{1,2},{2,3},{3,4},{4,5},{5,6},{6,7},{7,8},{8,9},{9,10},{10,1... | collective-permute-start | bytes 2359304 | tf_op jit(solution)/shard_map/ppermute | solution.py:28
  9.4 13.5 %collective-permute-start.1 = (f32[8,64,384]{2,1,0:T(8,128)}, f32[8,64,384]{2,1,0:T(8,128)S(1)}, u32[]{:S(2)}, u32[]{:S(2)}) collective-permute-start(f32[8,64,384]{2,1,0:T(8,128)} %shard_map.165.own_ref), channel_id=1, source_target_pairs={{1,0},{2,1},{3,2},{4,3},{5,4},{6,5},{7,6},{8,7},{9,8},{10,9},{11,1... | collective-permute-start | bytes 2359304 | tf_op jit(solution)/shard_map/ppermute | solution.py:28
  11.4 0.6 copy-start.9
  12.2 0.7 copy-start.7
  12.9 0.7 copy-start.10
  13.8 0.7 copy-start.4
  15.8 0.7 copy-start.11
  17.1 0.7 copy-start.12
  20.7 3.6 %copy-start = (f32[8,64,384]{2,1,0:T(8,128)}, f32[8,64,384]{2,1,0:T(8,128)S(1)}, u32[]{:S(2)}) copy-start(f32[8,64,384]{2,1,0:T(8,128)S(1)} %collective-permute-done.prev_ref) | copy-start | bytes 2359300
  22.9 1.5 copy-start.1
  33.4 11.1 %collective-permute-start.2 = (f32[8,64,384]{2,1,0:T(8,128)}, f32[8,64,384]{2,1,0:T(8,128)S(1)}, u32[]{:S(2)}, u32[]{:S(2)}) collective-permute-start(f32[8,64,384]{2,1,0:T(8,128)} %get-tuple-element.15.own_ref), channel_id=1, source_target_pairs={{0,1},{1,2},{2,3},{3,4},{4,5},{5,6},{6,7},{7,8},{8,9},{9,10},{10,1... | collective-permute-start | bytes 2359304 | tf_op jit(solution)/shard_map/ppermute | solution.py:28
  35.3 13.8 %collective-permute-start.3 = (f32[8,64,384]{2,1,0:T(8,128)}, f32[8,64,384]{2,1,0:T(8,128)S(1)}, u32[]{:S(2)}, u32[]{:S(2)}) collective-permute-start(f32[8,64,384]{2,1,0:T(8,128)} %get-tuple-element.15.own_ref), channel_id=1, source_target_pairs={{1,0},{2,1},{3,2},{4,3},{5,4},{6,5},{7,6},{8,7},{9,8},{10,9},{11,1... | collective-permute-start | bytes 2359304 | tf_op jit(solution)/shard_map/ppermute | solution.py:28
  44.5 4.6 %copy-start.2 = (f32[8,64,384]{2,1,0:T(8,128)}, f32[8,64,384]{2,1,0:T(8,128)S(1)}, u32[]{:S(2)}) copy-start(f32[8,64,384]{2,1,0:T(8,128)S(1)} %collective-permute-done.2.prev_ref) | copy-start | bytes 2359300
  49.1 0.9 copy-start.3
  60.2 31.8 %all-to-all-start = ((f32[128,1,384]{2,1,0:T(1,128)}), f32[128,1,384]{2,1,0:T(1,128)S(1)}, u32[]{:S(2)}, u32[]{:S(2)}) async-start(f32[128,1,384]{2,1,0:T(1,128)} %copy.47), calls=%async_computation | async-start | bytes 393216 | tf_op jit(solution)/shard_map/all_to_all | solution.py:527
  95.5 17.2 %all-to-all-start.1 = ((f32[256,1,8]{2,1,0:T(1,128)}), f32[256,1,8]{2,1,0:T(1,128)S(1)}, u32[]{:S(2)}, u32[]{:S(2)}) async-start(f32[256,1,8]{2,1,0:T(1,128)} %bitcast.52), calls=%async_computation.1 | async-start | bytes 262144 | tf_op jit(solution)/shard_map/all_to_all | solution.py:532
  120.1 0.7 copy-start.8
  147.0 6.3 %copy-start.5 = (f32[16,128]{1,0:T(8,128)S(1)}, f32[16,128]{1,0:T(8,128)}, u32[]{:S(2)}) copy-start(f32[16,128]{1,0:T(8,128)} %get-tuple-element.18) | copy-start | bytes 24580
  147.0 17.6 %all-to-all-start.3 = ((f32[128,1,256]{2,1,0:T(1,128)}), f32[128,1,256]{2,1,0:T(1,128)S(1)}, u32[]{:S(2)}, u32[]{:S(2)}) async-start(f32[128,1,256]{2,1,0:T(1,128)} %copy.57), calls=%async_computation.3 | async-start | bytes 262144 | tf_op jit(solution)/shard_map/all_to_all | solution.py:541
  153.3 0.7 copy-start.6

commit v3 on v2

--- a/solution.py
+++ b/solution.py
@@ -220,6 +220,12 @@
 INTERPRET = False
 
 
+def on_chip(*values):
+    if INTERPRET:
+        return values
+    return tuple(pltpu.with_memory_space_constraint(value, pltpu.VMEM) for value in values)
+
+
 def make_faces(state_in, selection):
     return pl.pallas_call(
         faces_kernel,
@@ -247,7 +253,12 @@
             pltpu.VMEM((variables, 64, 128), jnp.float32),
         ],
         interpret=INTERPRET,
-    )(mix, speeds, flow, state_in, prev, own, following, pick, expand, rate, selection, place, segment)
+    )(
+        mix,
+        speeds,
+        flow,
+        state_in, *on_chip(prev, own, following, pick, expand, rate, selection), place, segment,
+    )
 
 
 def block_picks(neighbours, offset):
@@ -364,7 +375,7 @@
         out_specs=tuple([VMEM_SPEC] * len(shapes)),
         scratch_shapes=[pltpu.VMEM(shape, jnp.float32) for shape in scratch],
         interpret=INTERPRET,
-    )(*operands)
+    )(*on_chip(*operands))
 
 
 def legendre_start(sine_lat, orders):
@@ -458,10 +469,7 @@
         coef_prev.reshape(-1),
         coef_before.reshape(-1),
         gain,
-        rows[0] * weights,
-        rows[1] * weights,
-        diagonal,
-        cosine,
+        *on_chip(rows[0] * weights, rows[1] * weights, diagonal, cosine),
     )
     both = jnp.stack([acc_re, acc_im]).reshape(2, 2, 4, 128)
     return both.transpose(1, 3, 0, 2).reshape(256, 8)

time: 168 us -> 165 us (0.982)
  Pallas kernels: 34.2 us -> 29.6 us
  other arithmetic: 9.92 us -> 7.08 us
  waiting for transfers between devices: 37.4 us -> 40.2 us
  local copies, waits for them, and re-layouts: 20.7 us -> 22.6 us
    pallas_call x3, Pallas kernels: 7.2 us -> 4.3 us  [run_kernel(): pl.pallas_call(kernel, out_shape=tuple((jax.ShapeDtypeStruct(shape, jnp.f...]
    ppermute x4, waiting for transfers between devices: 12.7 us -> 15.5 us  [passed_along(): lax.ppermute(value, axis, [(source, source + steps) for source in range(l...]
    unnamed x28 -> x58, local copies, waits for them, and re-layouts: 4.96 us -> 7.57 us
  transfers between devices with their start and end apart: 7 -> 7, of which waited for: 6 -> 7; matrix products, arithmetic and copies ran while one was open for 11% -> 10% of each run, Pallas kernels for 0% -> 0%
where the time goes in v3:
time: 165 us; the launch traced here: 164 us
  starting transfers between devices  43 us (26%)
  waiting for transfers between devices  40.2 us (24%)
  Pallas kernels  29.6 us (18%)
  local copies, waits for them, and re-layouts  22.6 us (14%)
  blocking collectives  20.5 us (12%)
  other arithmetic  7.08 us (4%)
    all_to_all x1, blocking collectives, body(): lax.all_to_all(synth, axes, split_axis=0, concat_axis=0, tiled=True)  20.5 us
    all_to_all x1, starting transfers between devices, body(): got = lax.all_to_all(faces, 'grp', split_axis=0, concat_axis=0, tiled=True)  20 us
    pallas_call x2, Pallas kernels, advance(): pl.pallas_call(functools.partial(step_kernel, last=last), out_shape=(jax....  15.8 us
    ppermute x4, waiting for transfers between devices, passed_along(): lax.ppermute(value, axis, [(source, source + steps) for source in range(l...  15.5 us
    ppermute x4, starting transfers between devices, passed_along(): lax.ppermute(value, axis, [(source, source + steps) for source in range(l...  11.5 us
    all_to_all x1, waiting for transfers between devices, body(): got = lax.all_to_all(faces, 'grp', split_axis=0, concat_axis=0, tiled=True)  9.91 us
    all_to_all x1, waiting for transfers between devices, body(): home = lax.all_to_all(back, 'grp', split_axis=0, concat_axis=0, tiled=True)  9.8 us
    unnamed x58, local copies, waits for them, and re-layouts  7.57 us
  transfers between devices with their start and end apart: 7, of which 7 were waited for; matrix products, arithmetic and copies ran while one was open for 10% of the time, Pallas kernels for 0%

profile of v3, /device:TPU:1, one launch (start us, length us, event | category | flops | bytes accessed | tf_op | source)
XLA Modules:
  0.0 164.0 jit_solution(11088648181874109844)
XLA Ops:
  1.5 3.0 %shard_map.165.own_ref = f32[8,64,384]{2,1,0:T(8,128)} custom-call(f32[8,64,512]{2,1,0:T(8,128)} %state_ref.3, bf16[512,256]{1,0:T(8,128)(2,1)} %fusion.15.select_ref), custom_call_target="tpu_custom_call" | custom-call | tf_op jit(solution)/shard_map/pallas_call | solution.py:230
  4.5 5.1 %collective-permute-start = (f32[8,64,384]{2,1,0:T(8,128)}, f32[8,64,384]{2,1,0:T(8,128)S(1)}, u32[]{:S(2)}, u32[]{:S(2)}) collective-permute-start(f32[8,64,384]{2,1,0:T(8,128)} %shard_map.165.own_ref), channel_id=1, source_target_pairs={{0,1},{1,2},{2,3},{3,4},{4,5},{5,6},{6,7},{7,8},{8,9},{9,10},{10,1... | collective-permute-start | bytes 2359304 | tf_op jit(solution)/shard_map/ppermute | solution.py:28
  9.6 1.9 %collective-permute-start.1 = (f32[8,64,384]{2,1,0:T(8,128)}, f32[8,64,384]{2,1,0:T(8,128)S(1)}, u32[]{:S(2)}, u32[]{:S(2)}) collective-permute-start(f32[8,64,384]{2,1,0:T(8,128)} %shard_map.165.own_ref), channel_id=1, source_target_pairs={{1,0},{2,1},{3,2},{4,3},{5,4},{6,5},{7,6},{8,7},{9,8},{10,9},{11,1... | collective-permute-start | bytes 2359304 | tf_op jit(solution)/shard_map/ppermute | solution.py:28
  18.8 4.3 %collective-permute-done.1.next_ref = f32[8,64,384]{2,1,0:T(8,128)S(1)} collective-permute-done((f32[8,64,384]{2,1,0:T(8,128)}, f32[8,64,384]{2,1,0:T(8,128)S(1)}, u32[]{:S(2)}, u32[]{:S(2)}) %collective-permute-start.1) | collective-permute-done | bytes 786464 | tf_op jit(solution)/shard_map/ppermute | solution.py:28
  23.9 8.3 %shard_map.166 = (f32[8,64,512]{2,1,0:T(8,128)}, f32[8,64,384]{2,1,0:T(8,128)}) custom-call(f32[192]{0:T(256)} %mul.173.mix_ref, f32[3]{0:T(128)} %broadcast_multiply_fusion.1.speed_ref, f32[8]{0:T(128)} %flow_ref.3, f32[8,64,512]{2,1,0:T(8,128)} %state_ref.3, f32[8,64,384]{2,1,0:T(8,128)S(1)} %collective-permute-done.prev_ref, f32[8,64,384]{2,1,0:T(8,128)S(1)} %copy-done.2, ...), custom_call_target="tpu_custom_call" | custom-call | tf_op jit(solution)/shard_map/pallas_call | solution.py:242
  32.2 2.0 %collective-permute-start.2 = (f32[8,64,384]{2,1,0:T(8,128)}, f32[8,64,384]{2,1,0:T(8,128)S(1)}, u32[]{:S(2)}, u32[]{:S(2)}) collective-permute-start(f32[8,64,384]{2,1,0:T(8,128)} %get-tuple-element.15.own_ref), channel_id=1, source_target_pairs={{0,1},{1,2},{2,3},{3,4},{4,5},{5,6},{6,7},{7,8},{8,9},{9,10},{10,1... | collective-permute-start | bytes 2359304 | tf_op jit(solution)/shard_map/ppermute | solution.py:28
  34.2 2.5 %collective-permute-start.3 = (f32[8,64,384]{2,1,0:T(8,128)}, f32[8,64,384]{2,1,0:T(8,128)S(1)}, u32[]{:S(2)}, u32[]{:S(2)}) collective-permute-start(f32[8,64,384]{2,1,0:T(8,128)} %get-tuple-element.15.own_ref), channel_id=1, source_target_pairs={{1,0},{2,1},{3,2},{4,3},{5,4},{6,5},{7,6},{8,7},{9,8},{10,9},{11,1... | collective-permute-start | bytes 2359304 | tf_op jit(solution)/shard_map/ppermute | solution.py:28
  36.8 6.6 %collective-permute-done.2.prev_ref = f32[8,64,384]{2,1,0:T(8,128)S(1)} collective-permute-done((f32[8,64,384]{2,1,0:T(8,128)}, f32[8,64,384]{2,1,0:T(8,128)S(1)}, u32[]{:S(2)}, u32[]{:S(2)}) %collective-permute-start.2) | collective-permute-done | bytes 786464 | tf_op jit(solution)/shard_map/ppermute | solution.py:28
  44.3 3.7 %collective-permute-done.3.next_ref = f32[8,64,384]{2,1,0:T(8,128)S(1)} collective-permute-done((f32[8,64,384]{2,1,0:T(8,128)}, f32[8,64,384]{2,1,0:T(8,128)S(1)}, u32[]{:S(2)}, u32[]{:S(2)}) %collective-permute-start.3) | collective-permute-done | bytes 786464 | tf_op jit(solution)/shard_map/ppermute | solution.py:28
  50.0 1.1 copy-done.7
  53.4 7.5 %shard_map.167 = (f32[8,64,512]{2,1,0:T(8,128)}, f32[128,384]{1,0:T(8,128)}) custom-call(f32[192]{0:T(256)} %mul.173.mix_ref, f32[3]{0:T(128)} %broadcast_multiply_fusion.1.speed_ref, f32[8]{0:T(128)} %flow_ref.3, f32[8,64,512]{2,1,0:T(8,128)} %get-tuple-element.14.state_ref, f32[8,64,384]{2,1,0:T(8,128)S(1)} %copy-done.9, f32[8,64,384]{2,1,0:T(8,128)S(1)} %copy-done.7, ...), custom_call_target="tpu_custom_call" | custom-call | tf_op jit(solution)/shard_map/pallas_call | solution.py:242
  60.8 1.8 %copy.47 = f32[128,1,384]{2,1,0:T(1,128)} copy(f32[128,1,384]{2,0,1:T(8,128)} %bitcast.51) | data formatting | bytes 393216 | tf_op jit(solution)/shard_map/all_to_all | solution.py:535
  62.6 20.0 %all-to-all-start = ((f32[128,1,384]{2,1,0:T(1,128)}), f32[128,1,384]{2,1,0:T(1,128)S(1)}, u32[]{:S(2)}, u32[]{:S(2)}) async-start(f32[128,1,384]{2,1,0:T(1,128)} %copy.47), calls=%async_computation | async-start | bytes 393216 | tf_op jit(solution)/shard_map/all_to_all | solution.py:535
  84.5 9.9 %all-to-all-done = f32[128,1,384]{2,1,0:T(1,128)S(1)} async-done(((f32[128,1,384]{2,1,0:T(1,128)}), f32[128,1,384]{2,1,0:T(1,128)S(1)}, u32[]{:S(2)}, u32[]{:S(2)}) %all-to-all-start) | async-done | bytes 196640 | tf_op jit(solution)/shard_map/all_to_all | solution.py:535
  94.5 1.9 %shard_map.168 = (f32[16,128]{1,0:T(8,128)}, f32[256,8]{1,0:T(8,128)}) custom-call(f32[128,384]{1,0:T(8,128)S(1)} %bitcast.47, f32[16,128]{1,0:T(8,128)S(1)} %copy-done.18, f32[2,64,64]{2,1,0:T(8,128)S(1)} %copy-done.13, f32[32,128]{1,0:T(8,128)S(1)} %copy-done.17), custom_call_target="tpu_custom_call" | custom-call | tf_op jit(solution)/shard_map/pallas_call | solution.py:371
  96.3 5.3 %all-to-all-start.1 = ((f32[256,1,8]{2,1,0:T(1,128)}), f32[256,1,8]{2,1,0:T(1,128)S(1)}, u32[]{:S(2)}, u32[]{:S(2)}) async-start(f32[256,1,8]{2,1,0:T(1,128)} %bitcast.52), calls=%async_computation.1 | async-start | bytes 262144 | tf_op jit(solution)/shard_map/all_to_all | solution.py:540
  101.7 6.9 %gather_fusion = f32[1024]{0:T(1024)S(1)} fusion(f32[512]{0:T(512)S(1)} %pad_maximum_fusion.1, s32[1024]{0:T(1024)S(1)} %bitcast_clamp_fusion), kind=kCustom, calls=%fused_computation | custom fusion | bytes 12288 | tf_op jit(solution)/shard_map/jit(_take)/gather | solution.py:389
  108.5 5.0 %all-to-all-done.1 = f32[256,1,8]{2,1,0:T(1,128)S(1)} async-done(((f32[256,1,8]{2,1,0:T(1,128)}), f32[256,1,8]{2,1,0:T(1,128)S(1)}, u32[]{:S(2)}, u32[]{:S(2)}) %all-to-all-start.1) | async-done | bytes 8224 | tf_op jit(solution)/shard_map/all_to_all | solution.py:540
  113.7 6.5 %shard_map.169 = (f32[8,128]{1,0:T(8,128)}, f32[8,128]{1,0:T(8,128)}) custom-call(s32[1]{0:T(128)} %bitcast.63, f32[1024]{0:T(1024)} %get-tuple-element.31.prev_ref, f32[1024]{0:T(1024)} %get-tuple-element.30.before_ref, f32[512]{0:T(512)} %fusion.35.gain_ref, f32[8,128]{1,0:T(8,128)S(1)} %get-tuple-element.34.re_ref, ...), custom_call_target="tpu_custom_call" | custom-call | tf_op jit(solution)/shard_map/pallas_call | solution.py:461
  121.8 20.5 %all_to_all.42 = f32[256,1,8]{2,1,0:T(1,128)S(1)} all-to-all(f32[256,1,8]{2,1,0:T(1,128)S(1)} %copy.55), channel_id=1, replica_groups=mesh['grp'=128,'cores'=2] {'grp','cores'}, dimensions={0} | all-to-all | bytes 16384 | tf_op jit(solution)/shard_map/all_to_all | solution.py:542
  142.3 1.6 shard_map.170
  143.8 1.7 %copy.57 = f32[128,1,256]{2,1,0:T(1,128)} copy(f32[128,1,256]{2,0,1:T(8,128)} %bitcast.53) | data formatting | bytes 262144 | tf_op jit(solution)/shard_map/all_to_all | solution.py:549
  145.5 6.3 %all-to-all-start.3 = ((f32[128,1,256]{2,1,0:T(1,128)}), f32[128,1,256]{2,1,0:T(1,128)S(1)}, u32[]{:S(2)}, u32[]{:S(2)}) async-start(f32[128,1,256]{2,1,0:T(1,128)} %copy.57), calls=%async_computation.3 | async-start | bytes 262144 | tf_op jit(solution)/shard_map/all_to_all | solution.py:549
  153.4 9.8 %all-to-all-done.3 = f32[128,1,256]{2,1,0:T(1,128)S(1)} async-done(((f32[128,1,256]{2,1,0:T(1,128)}), f32[128,1,256]{2,1,0:T(1,128)S(1)}, u32[]{:S(2)}, u32[]{:S(2)}) %all-to-all-start.3) | async-done | bytes 131104 | tf_op jit(solution)/shard_map/all_to_all | solution.py:549
  (131 shorter events, 19.9 us)
Async XLA Ops:
  1.4 11.5 %copy-start.22 = (s32[64,6]{0,1:T(8,128)S(1)}, s32[64,6]{0,1:T(8,128)}, u32[]{:S(2)}) copy-start(s32[64,6]{0,1:T(8,128)} %param.17) | copy-start | bytes 4612
  1.4 11.6 %copy-start.25 = (s32[64,1]{0,1:T(1,128)S(1)}, s32[64,1]{0,1:T(1,128)}, u32[]{:S(2)}) copy-start(s32[64,1]{0,1:T(1,128)} %param.18) | copy-start | bytes 772
  1.4 12.4 %copy-start.19 = (f32[3,8,8]{2,1,0:T(8,128)S(1)}, f32[3,8,8]{2,1,0:T(8,128)}, u32[]{:S(2)}) copy-start(f32[3,8,8]{2,1,0:T(8,128)} %param.15) | copy-start | bytes 2308
  1.5 14.4 %copy-start.26 = (s32[64]{0:T(128)S(1)}, s32[64]{0:T(128)}, u32[]{:S(2)}) copy-start(s32[64]{0:T(128)} %param.19) | copy-start | bytes 772
  1.5 15.0 %copy-start.27 = (s32[64]{0:T(128)S(1)}, s32[64]{0:T(128)}, u32[]{:S(2)}) copy-start(s32[64]{0:T(128)} %param.16) | copy-start | bytes 772
  4.5 19.3 %copy-start.2 = (f32[8,64,384]{2,1,0:T(8,128)S(1)}, f32[8,64,384]{2,1,0:T(8,128)}, u32[]{:S(2)}) copy-start(f32[8,64,384]{2,1,0:T(8,128)} %shard_map.165.own_ref) | copy-start | bytes 2359300
  4.5 14.3 %collective-permute-start = (f32[8,64,384]{2,1,0:T(8,128)}, f32[8,64,384]{2,1,0:T(8,128)S(1)}, u32[]{:S(2)}, u32[]{:S(2)}) collective-permute-start(f32[8,64,384]{2,1,0:T(8,128)} %shard_map.165.own_ref), channel_id=1, source_target_pairs={{0,1},{1,2},{2,3},{3,4},{4,5},{5,6},{6,7},{7,8},{8,9},{9,10},{10,1... | collective-permute-start | bytes 2359304 | tf_op jit(solution)/shard_map/ppermute | solution.py:28
  9.6 13.5 %collective-permute-start.1 = (f32[8,64,384]{2,1,0:T(8,128)}, f32[8,64,384]{2,1,0:T(8,128)S(1)}, u32[]{:S(2)}, u32[]{:S(2)}) collective-permute-start(f32[8,64,384]{2,1,0:T(8,128)} %shard_map.165.own_ref), channel_id=1, source_target_pairs={{1,0},{2,1},{3,2},{4,3},{5,4},{6,5},{7,6},{8,7},{9,8},{10,9},{11,1... | collective-permute-start | bytes 2359304 | tf_op jit(solution)/shard_map/ppermute | solution.py:28
  17.4 6.4 %copy-start.4 = (bf16[3,128,256]{2,1,0:T(8,128)(2,1)}, bf16[3,128,256]{2,1,0:T(8,128)(2,1)S(1)}, u32[]{:S(2)}) copy-start(bf16[3,128,256]{2,1,0:T(8,128)(2,1)S(1)} %fusion.16.pick_ref) | copy-start | bytes 589828
  17.9 14.2 %copy-start = (bf16[2,256,512]{2,1,0:T(8,128)(2,1)}, bf16[2,256,512]{2,1,0:T(8,128)(2,1)S(1)}, u32[]{:S(2)}) copy-start(bf16[2,256,512]{2,1,0:T(8,128)(2,1)S(1)} %fusion.9.expand_ref) | copy-start | bytes 1572868
  32.1 16.8 %copy-start.5 = (bf16[3,128,256]{2,1,0:T(8,128)(2,1)S(1)}, bf16[3,128,256]{2,1,0:T(8,128)(2,1)}, u32[]{:S(2)}) copy-start(bf16[3,128,256]{2,1,0:T(8,128)(2,1)} %copy-done.4) | copy-start | bytes 589828
  32.2 11.3 %collective-permute-start.2 = (f32[8,64,384]{2,1,0:T(8,128)}, f32[8,64,384]{2,1,0:T(8,128)S(1)}, u32[]{:S(2)}, u32[]{:S(2)}) collective-permute-start(f32[8,64,384]{2,1,0:T(8,128)} %get-tuple-element.15.own_ref), channel_id=1, source_target_pairs={{0,1},{1,2},{2,3},{3,4},{4,5},{5,6},{6,7},{7,8},{8,9},{9,10},{10,1... | collective-permute-start | bytes 2359304 | tf_op jit(solution)/shard_map/ppermute | solution.py:28
  34.2 13.8 %collective-permute-start.3 = (f32[8,64,384]{2,1,0:T(8,128)}, f32[8,64,384]{2,1,0:T(8,128)S(1)}, u32[]{:S(2)}, u32[]{:S(2)}) collective-permute-start(f32[8,64,384]{2,1,0:T(8,128)} %get-tuple-element.15.own_ref), channel_id=1, source_target_pairs={{1,0},{2,1},{3,2},{4,3},{5,4},{6,5},{7,6},{8,7},{9,8},{10,9},{11,1... | collective-permute-start | bytes 2359304 | tf_op jit(solution)/shard_map/ppermute | solution.py:28
  62.6 31.8 %all-to-all-start = ((f32[128,1,384]{2,1,0:T(1,128)}), f32[128,1,384]{2,1,0:T(1,128)S(1)}, u32[]{:S(2)}, u32[]{:S(2)}) async-start(f32[128,1,384]{2,1,0:T(1,128)} %copy.47), calls=%async_computation | async-start | bytes 393216 | tf_op jit(solution)/shard_map/all_to_all | solution.py:535
  84.5 9.9 %copy-start.13 = (f32[2,64,64]{2,1,0:T(8,128)S(1)}, f32[2,64,64]{2,1,0:T(8,128)}, u32[]{:S(2)}) copy-start(f32[2,64,64]{2,1,0:T(8,128)} %constant.296.clone.twiddle_ref) | copy-start | bytes 98308
  84.5 9.9 %copy-start.17 = (f32[32,128]{1,0:T(8,128)S(1)}, f32[32,128]{1,0:T(8,128)}, u32[]{:S(2)}) copy-start(f32[32,128]{1,0:T(8,128)} %constant.297.clone.forward_ref) | copy-start | bytes 49156
  84.5 10.0 %copy-start.18 = (f32[16,128]{1,0:T(8,128)S(1)}, f32[16,128]{1,0:T(8,128)}, u32[]{:S(2)}) copy-start(f32[16,128]{1,0:T(8,128)} %constant.295.clone.split_ref) | copy-start | bytes 24580
  96.3 17.2 %all-to-all-start.1 = ((f32[256,1,8]{2,1,0:T(1,128)}), f32[256,1,8]{2,1,0:T(1,128)S(1)}, u32[]{:S(2)}, u32[]{:S(2)}) async-start(f32[256,1,8]{2,1,0:T(1,128)} %bitcast.52), calls=%async_computation.1 | async-start | bytes 262144 | tf_op jit(solution)/shard_map/all_to_all | solution.py:540
  121.7 20.5 %copy-start.12 = (f32[2,64,64]{2,1,0:T(8,128)S(1)}, f32[2,64,64]{2,1,0:T(8,128)}, u32[]{:S(2)}) copy-start(f32[2,64,64]{2,1,0:T(8,128)} %constant.300.clone.untwist_ref) | copy-start | bytes 98308
  121.7 20.5 %copy-start.14 = (f32[64,64]{1,0:T(8,128)S(1)}, f32[64,64]{1,0:T(8,128)}, u32[]{:S(2)}) copy-start(f32[64,64]{1,0:T(8,128)} %constant.299.clone.backward_ref) | copy-start | bytes 49156
  121.8 20.5 %copy-start.15 = (f32[32,64]{1,0:T(8,128)S(1)}, f32[32,64]{1,0:T(8,128)}, u32[]{:S(2)}) copy-start(f32[32,64]{1,0:T(8,128)} %constant.298.clone.factor_ref) | copy-start | bytes 24580
  121.8 20.5 %copy-start.16 = (f32[32,128]{1,0:T(8,128)S(1)}, f32[32,128]{1,0:T(8,128)}, u32[]{:S(2)}) copy-start(f32[32,128]{1,0:T(8,128)} %constant.301.clone.join_ref) | copy-start | bytes 49156
  145.5 17.6 %all-to-all-start.3 = ((f32[128,1,256]{2,1,0:T(1,128)}), f32[128,1,256]{2,1,0:T(1,128)S(1)}, u32[]{:S(2)}, u32[]{:S(2)}) async-start(f32[128,1,256]{2,1,0:T(1,128)} %copy.57), calls=%async_computation.3 | async-start | bytes 262144 | tf_op jit(solution)/shard_map/all_to_all | solution.py:549
  153.4 9.8 %copy-start.6 = (bf16[2,128,64]{2,1,0:T(8,128)(2,1)S(1)}, bf16[2,128,64]{2,1,0:T(8,128)(2,1)}, u32[]{:S(2)}) copy-start(bf16[2,128,64]{2,1,0:T(8,128)(2,1)} %fusion.19.place_ref) | copy-start | bytes 98308
  (11 other events, 20.9 us)

commit v4 on v3

--- a/solution.py
+++ b/solution.py
@@ -205,10 +205,10 @@
         parts = jnp.concatenate(split_three(patches) + (segment_ref[...],), axis=1)
         sent = [product(place_ref[0], parts), product(place_ref[1], parts)]
         for k in range(2):
-            extra_ref[:, 128 * k : 128 * k + 128] = sum_of_parts(
+            extra_ref[:, 0, 128 * k : 128 * k + 128] = sum_of_parts(
                 [sent[k][:, 128 * i : 128 * i + 128] for i in range(3)]
             )
-        extra_ref[:, 256:384] = jnp.where(
+        extra_ref[:, 0, 256:384] = jnp.where(
             iota((128, 128), 1) < 64, sent[0][:, 384:512], sent[1][:, 384:512]
         )
     else:
@@ -238,7 +238,11 @@
 
 def advance(mix, speeds, flow, state_in, prev, own, following, pick, expand, rate, selection, place, segment, last):
     variables, blocks = state_in.shape[:2]
-    extra = (128, 384) if last else (variables, blocks, 384)
+    (prev, following), shared = on_chip(prev, following), (pick, expand, rate, selection)
+    if not last:
+        own, *shared = on_chip(own, *shared)
+    operands = (state_in, prev, own, following, *shared, place, segment)
+    extra = (128, 1, 384) if last else (variables, blocks, 384)
     return pl.pallas_call(
         functools.partial(step_kernel, last=last),
         out_shape=(
@@ -257,7 +261,7 @@
         mix,
         speeds,
         flow,
-        state_in, *on_chip(prev, own, following, pick, expand, rate, selection), place, segment,
+        *operands,
     )
 
 
@@ -350,7 +354,7 @@
     codes = got_ref[:, 256:384]
     for k in range(2):
         found = product(landing_of(codes, k).astype(jnp.float32).astype(jnp.bfloat16), parts)
-        back_ref[:, 128 * k : 128 * k + 128] = sum_of_parts(
+        back_ref[:, 0, 128 * k : 128 * k + 128] = sum_of_parts(
             [found[:, 128 * i : 128 * i + 128] for i in range(3)]
         )
 
@@ -533,6 +537,7 @@
         )
     split, twiddle, forward, factor, backward, untwist, join = transform_tables()
     got = lax.all_to_all(faces, "grp", split_axis=0, concat_axis=0, tiled=True)
+    got = got.reshape(grp_size, 384)
     fac_segments, coef = run_kernel(
         forward_kernel, (got, split, twiddle, forward), ((16, 128), (device_total, 8))
     )
@@ -543,10 +548,11 @@
     grid_segments, back = run_kernel(
         backward_kernel,
         (returned, got, factor, backward, untwist, join),
-        ((16, 128), (grp_size, 256)),
+        ((16, 128), (grp_size, 1, 256)),
         scratch=((64, 64),),
     )
     home = lax.all_to_all(back, "grp", split_axis=0, concat_axis=0, tiled=True)
+    home = home.reshape(grp_size, 256)
     (shell_potential,) = run_kernel(home_kernel, (home, place), ((block_portion, 128),))
     fac_local, potential_local = (
         jnp.swapaxes(grid.reshape(16, LAT_DEV, 64), 0, 1).reshape(LAT_DEV, NLON)

time: 165 us -> 156 us (0.945)
  local copies, waits for them, and re-layouts: 22.6 us -> 12.8 us
    unnamed x58 -> x46, local copies, waits for them, and re-layouts: 7.57 us -> 1.31 us
    all_to_all x2 -> x0, local copies, waits for them, and re-layouts: 3.48 us -> none  [the longest x1 1.8 us: body(): got = lax.all_to_all(faces, 'grp', split_axis=0, concat_axis=0, tiled=True)]
  transfers between devices with their start and end apart: 7 -> 7, of which waited for: 7 -> 7; matrix products, arithmetic and copies ran while one was open for 10% -> 11% of each run, Pallas kernels for 0% -> 0%
where the time goes in v4:
time: 156 us; the launch traced here: 155 us
  starting transfers between devices  42.7 us (27%)
  waiting for transfers between devices  40.6 us (26%)
  Pallas kernels  30.1 us (19%)
  blocking collectives  20.4 us (13%)
  local copies, waits for them, and re-layouts  12.8 us (8%)
  other arithmetic  7.74 us (5%)
    all_to_all x1, blocking collectives, body(): lax.all_to_all(synth, axes, split_axis=0, concat_axis=0, tiled=True)  20.4 us
    all_to_all x1, starting transfers between devices, body(): got = lax.all_to_all(faces, 'grp', split_axis=0, concat_axis=0, tiled=True)  20 us
    pallas_call x2, Pallas kernels, advance(): pl.pallas_call(functools.partial(step_kernel, last=last), out_shape=(jax....  16.3 us
    ppermute x4, waiting for transfers between devices, passed_along(): lax.ppermute(value, axis, [(source, source + steps) for source in range(l...  15.7 us
    ppermute x4, starting transfers between devices, passed_along(): lax.ppermute(value, axis, [(source, source + steps) for source in range(l...  11.3 us
    all_to_all x1, waiting for transfers between devices, body(): got = lax.all_to_all(faces, 'grp', split_axis=0, concat_axis=0, tiled=True)  9.91 us
    all_to_all x1, waiting for transfers between devices, body(): home = lax.all_to_all(back, 'grp', split_axis=0, concat_axis=0, tiled=True)  9.79 us
    gather x1, local copies, waits for them, and re-layouts, legendre_start(): log_base = jnp.take(log_sums, orders)  6.87 us
  transfers between devices with their start and end apart: 7, of which 7 were waited for; matrix products, arithmetic and copies ran while one was open for 11% of the time, Pallas kernels for 0%

profile of v4, /device:TPU:1, one launch (start us, length us, event | category | flops | bytes accessed | tf_op | source)
XLA Modules:
  0.0 155.5 jit_solution(6672365999305655523)
XLA Ops:
  0.7 0.8 fusion.15.select_ref
  1.5 3.0 %shard_map.165.own_ref = f32[8,64,384]{2,1,0:T(8,128)} custom-call(f32[8,64,512]{2,1,0:T(8,128)} %state_ref.3, bf16[512,256]{1,0:T(8,128)(2,1)} %fusion.15.select_ref), custom_call_target="tpu_custom_call" | custom-call | tf_op jit(solution)/shard_map/pallas_call | solution.py:230
  4.5 5.1 %collective-permute-start = (f32[8,64,384]{2,1,0:T(8,128)}, f32[8,64,384]{2,1,0:T(8,128)S(1)}, u32[]{:S(2)}, u32[]{:S(2)}) collective-permute-start(f32[8,64,384]{2,1,0:T(8,128)} %shard_map.165.own_ref), channel_id=1, source_target_pairs={{0,1},{1,2},{2,3},{3,4},{4,5},{5,6},{6,7},{7,8},{8,9},{9,10},{10,1... | collective-permute-start | bytes 2359304 | tf_op jit(solution)/shard_map/ppermute | solution.py:28
  9.6 1.9 %collective-permute-start.1 = (f32[8,64,384]{2,1,0:T(8,128)}, f32[8,64,384]{2,1,0:T(8,128)S(1)}, u32[]{:S(2)}, u32[]{:S(2)}) collective-permute-start(f32[8,64,384]{2,1,0:T(8,128)} %shard_map.165.own_ref), channel_id=1, source_target_pairs={{1,0},{2,1},{3,2},{4,3},{5,4},{6,5},{7,6},{8,7},{9,8},{10,9},{11,1... | collective-permute-start | bytes 2359304 | tf_op jit(solution)/shard_map/ppermute | solution.py:28
  17.9 0.9 collective-permute-done.prev_ref
  18.8 4.3 %collective-permute-done.1.next_ref = f32[8,64,384]{2,1,0:T(8,128)S(1)} collective-permute-done((f32[8,64,384]{2,1,0:T(8,128)}, f32[8,64,384]{2,1,0:T(8,128)S(1)}, u32[]{:S(2)}, u32[]{:S(2)}) %collective-permute-start.1) | collective-permute-done | bytes 786464 | tf_op jit(solution)/shard_map/ppermute | solution.py:28
  23.8 8.3 %shard_map.166 = (f32[8,64,512]{2,1,0:T(8,128)}, f32[8,64,384]{2,1,0:T(8,128)}) custom-call(f32[192]{0:T(256)} %mul.173.mix_ref, f32[3]{0:T(128)} %broadcast_multiply_fusion.1.speed_ref, f32[8]{0:T(128)} %flow_ref.3, f32[8,64,512]{2,1,0:T(8,128)} %state_ref.3, f32[8,64,384]{2,1,0:T(8,128)S(1)} %collective-permute-done.prev_ref, f32[8,64,384]{2,1,0:T(8,128)S(1)} %copy-done.1, ...), custom_call_target="tpu_custom_call" | custom-call | tf_op jit(solution)/shard_map/pallas_call | solution.py:246
  32.2 1.9 %collective-permute-start.2 = (f32[8,64,384]{2,1,0:T(8,128)}, f32[8,64,384]{2,1,0:T(8,128)S(1)}, u32[]{:S(2)}, u32[]{:S(2)}) collective-permute-start(f32[8,64,384]{2,1,0:T(8,128)} %get-tuple-element.15.own_ref), channel_id=1, source_target_pairs={{0,1},{1,2},{2,3},{3,4},{4,5},{5,6},{6,7},{7,8},{8,9},{9,10},{10,1... | collective-permute-start | bytes 2359304 | tf_op jit(solution)/shard_map/ppermute | solution.py:28
  34.1 2.5 %collective-permute-start.3 = (f32[8,64,384]{2,1,0:T(8,128)}, f32[8,64,384]{2,1,0:T(8,128)S(1)}, u32[]{:S(2)}, u32[]{:S(2)}) collective-permute-start(f32[8,64,384]{2,1,0:T(8,128)} %get-tuple-element.15.own_ref), channel_id=1, source_target_pairs={{1,0},{2,1},{3,2},{4,3},{5,4},{6,5},{7,6},{8,7},{9,8},{10,9},{11,1... | collective-permute-start | bytes 2359304 | tf_op jit(solution)/shard_map/ppermute | solution.py:28
  37.4 6.0 %collective-permute-done.2.prev_ref = f32[8,64,384]{2,1,0:T(8,128)S(1)} collective-permute-done((f32[8,64,384]{2,1,0:T(8,128)}, f32[8,64,384]{2,1,0:T(8,128)S(1)}, u32[]{:S(2)}, u32[]{:S(2)}) %collective-permute-start.2) | collective-permute-done | bytes 786464 | tf_op jit(solution)/shard_map/ppermute | solution.py:28
  43.3 4.6 %collective-permute-done.3.next_ref = f32[8,64,384]{2,1,0:T(8,128)S(1)} collective-permute-done((f32[8,64,384]{2,1,0:T(8,128)}, f32[8,64,384]{2,1,0:T(8,128)S(1)}, u32[]{:S(2)}, u32[]{:S(2)}) %collective-permute-start.3) | collective-permute-done | bytes 786464 | tf_op jit(solution)/shard_map/ppermute | solution.py:28
  47.9 8.0 %shard_map.167 = (f32[8,64,512]{2,1,0:T(8,128)}, f32[128,1,384]{2,1,0:T(1,128)}) custom-call(f32[192]{0:T(256)} %mul.173.mix_ref, f32[3]{0:T(128)} %broadcast_multiply_fusion.1.speed_ref, f32[8]{0:T(128)} %flow_ref.3, f32[8,64,512]{2,1,0:T(8,128)} %get-tuple-element.14.state_ref, f32[8,64,384]{2,1,0:T(8,128)S(1)} %collective-permute-done.2.prev_ref, ...), custom_call_target="tpu_custom_call" | custom-call | tf_op jit(solution)/shard_map/pallas_call | solution.py:246
  55.9 20.0 %all-to-all-start = ((f32[128,1,384]{2,1,0:T(1,128)}), f32[128,1,384]{2,1,0:T(1,128)S(1)}, u32[]{:S(2)}, u32[]{:S(2)}) async-start(f32[128,1,384]{2,1,0:T(1,128)} %get-tuple-element.17), calls=%async_computation | async-start | bytes 393216 | tf_op jit(solution)/shard_map/all_to_all | solution.py:539
  77.7 9.9 %all-to-all-done = f32[128,1,384]{2,1,0:T(1,128)S(1)} async-done(((f32[128,1,384]{2,1,0:T(1,128)}), f32[128,1,384]{2,1,0:T(1,128)S(1)}, u32[]{:S(2)}, u32[]{:S(2)}) %all-to-all-start) | async-done | bytes 196640 | tf_op jit(solution)/shard_map/all_to_all | solution.py:539
  87.7 1.9 %shard_map.168 = (f32[16,128]{1,0:T(8,128)}, f32[256,8]{1,0:T(8,128)}) custom-call(f32[128,384]{1,0:T(8,128)S(1)} %bitcast.45, f32[16,128]{1,0:T(8,128)S(1)} %copy-done.12, f32[2,64,64]{2,1,0:T(8,128)S(1)} %copy-done.7, f32[32,128]{1,0:T(8,128)S(1)} %copy-done.11), custom_call_target="tpu_custom_call" | custom-call | tf_op jit(solution)/shard_map/pallas_call | solution.py:375
  89.6 5.1 %all-to-all-start.1 = ((f32[256,1,8]{2,1,0:T(1,128)}), f32[256,1,8]{2,1,0:T(1,128)S(1)}, u32[]{:S(2)}, u32[]{:S(2)}) async-start(f32[256,1,8]{2,1,0:T(1,128)} %bitcast.49), calls=%async_computation.1 | async-start | bytes 262144 | tf_op jit(solution)/shard_map/all_to_all | solution.py:545
  94.7 6.9 %gather_fusion = f32[1024]{0:T(1024)S(1)} fusion(f32[512]{0:T(512)S(1)} %pad_maximum_fusion.1, s32[1024]{0:T(1024)S(1)} %bitcast_clamp_fusion), kind=kCustom, calls=%fused_computation | custom fusion | bytes 12288 | tf_op jit(solution)/shard_map/jit(_take)/gather | solution.py:393
  101.6 5.2 %all-to-all-done.1 = f32[256,1,8]{2,1,0:T(1,128)S(1)} async-done(((f32[256,1,8]{2,1,0:T(1,128)}), f32[256,1,8]{2,1,0:T(1,128)S(1)}, u32[]{:S(2)}, u32[]{:S(2)}) %all-to-all-start.1) | async-done | bytes 8224 | tf_op jit(solution)/shard_map/all_to_all | solution.py:545
  107.0 6.4 %shard_map.169 = (f32[8,128]{1,0:T(8,128)}, f32[8,128]{1,0:T(8,128)}) custom-call(s32[1]{0:T(128)} %bitcast.59, f32[1024]{0:T(1024)} %get-tuple-element.31.prev_ref, f32[1024]{0:T(1024)} %get-tuple-element.30.before_ref, f32[512]{0:T(512)} %fusion.35.gain_ref, f32[8,128]{1,0:T(8,128)S(1)} %get-tuple-element.34.re_ref, ...), custom_call_target="tpu_custom_call" | custom-call | tf_op jit(solution)/shard_map/pallas_call | solution.py:465
  114.9 20.4 %all_to_all.30 = f32[256,1,8]{2,1,0:T(1,128)S(1)} all-to-all(f32[256,1,8]{2,1,0:T(1,128)S(1)} %copy.54), channel_id=1, replica_groups=mesh['grp'=128,'cores'=2] {'grp','cores'}, dimensions={0} | all-to-all | bytes 16384 | tf_op jit(solution)/shard_map/all_to_all | solution.py:547
  135.4 1.6 %shard_map.170 = (f32[16,128]{1,0:T(8,128)}, f32[128,1,256]{2,1,0:T(1,128)}) custom-call(f32[256,8]{1,0:T(8,128)S(1)} %bitcast.47, f32[128,384]{1,0:T(8,128)S(1)} %bitcast.46, f32[32,64]{1,0:T(8,128)S(1)} %copy-done.9, f32[64,64]{1,0:T(8,128)S(1)} %copy-done.8, f32[2,64,64]{2,1,0:T(8,128)S(1)} %copy-done.6, f32[32,128]{1,0:T(8,128)S(1)} %copy-done.10), custom_call_target="tpu_custom_call" | custom-call | tf_op jit(solution)/shard_map/pallas_call | solution.py:375
  137.0 6.3 %all-to-all-start.3 = ((f32[128,1,256]{2,1,0:T(1,128)}), f32[128,1,256]{2,1,0:T(1,128)S(1)}, u32[]{:S(2)}, u32[]{:S(2)}) async-start(f32[128,1,256]{2,1,0:T(1,128)} %get-tuple-element.23), calls=%async_computation.3 | async-start | bytes 262144 | tf_op jit(solution)/shard_map/all_to_all | solution.py:554
  144.9 9.8 %all-to-all-done.3 = f32[128,1,256]{2,1,0:T(1,128)S(1)} async-done(((f32[128,1,256]{2,1,0:T(1,128)}), f32[128,1,256]{2,1,0:T(1,128)S(1)}, u32[]{:S(2)}, u32[]{:S(2)}) %all-to-all-start.3) | async-done | bytes 131104 | tf_op jit(solution)/shard_map/all_to_all | solution.py:554
  154.7 0.8 shard_map.171
  (117 shorter events, 12.9 us)
Async XLA Ops:
  1.4 11.5 %copy-start.16 = (s32[64,6]{0,1:T(8,128)S(1)}, s32[64,6]{0,1:T(8,128)}, u32[]{:S(2)}) copy-start(s32[64,6]{0,1:T(8,128)} %param.17) | copy-start | bytes 4612
  1.4 11.6 %copy-start.19 = (s32[64,1]{0,1:T(1,128)S(1)}, s32[64,1]{0,1:T(1,128)}, u32[]{:S(2)}) copy-start(s32[64,1]{0,1:T(1,128)} %param.18) | copy-start | bytes 772
  1.4 12.4 %copy-start.13 = (f32[3,8,8]{2,1,0:T(8,128)S(1)}, f32[3,8,8]{2,1,0:T(8,128)}, u32[]{:S(2)}) copy-start(f32[3,8,8]{2,1,0:T(8,128)} %param.15) | copy-start | bytes 2308
  1.4 14.3 %copy-start.20 = (s32[64]{0:T(128)S(1)}, s32[64]{0:T(128)}, u32[]{:S(2)}) copy-start(s32[64]{0:T(128)} %param.19) | copy-start | bytes 772
  1.4 15.0 %copy-start.21 = (s32[64]{0:T(128)S(1)}, s32[64]{0:T(128)}, u32[]{:S(2)}) copy-start(s32[64]{0:T(128)} %param.16) | copy-start | bytes 772
  4.5 19.3 %copy-start.1 = (f32[8,64,384]{2,1,0:T(8,128)S(1)}, f32[8,64,384]{2,1,0:T(8,128)}, u32[]{:S(2)}) copy-start(f32[8,64,384]{2,1,0:T(8,128)} %shard_map.165.own_ref) | copy-start | bytes 2359300
  4.5 14.3 %collective-permute-start = (f32[8,64,384]{2,1,0:T(8,128)}, f32[8,64,384]{2,1,0:T(8,128)S(1)}, u32[]{:S(2)}, u32[]{:S(2)}) collective-permute-start(f32[8,64,384]{2,1,0:T(8,128)} %shard_map.165.own_ref), channel_id=1, source_target_pairs={{0,1},{1,2},{2,3},{3,4},{4,5},{5,6},{6,7},{7,8},{8,9},{9,10},{10,1... | collective-permute-start | bytes 2359304 | tf_op jit(solution)/shard_map/ppermute | solution.py:28
  9.6 13.5 %collective-permute-start.1 = (f32[8,64,384]{2,1,0:T(8,128)}, f32[8,64,384]{2,1,0:T(8,128)S(1)}, u32[]{:S(2)}, u32[]{:S(2)}) collective-permute-start(f32[8,64,384]{2,1,0:T(8,128)} %shard_map.165.own_ref), channel_id=1, source_target_pairs={{1,0},{2,1},{3,2},{4,3},{5,4},{6,5},{7,6},{8,7},{9,8},{10,9},{11,1... | collective-permute-start | bytes 2359304 | tf_op jit(solution)/shard_map/ppermute | solution.py:28
  17.4 6.5 %copy-start.3 = (bf16[3,128,256]{2,1,0:T(8,128)(2,1)}, bf16[3,128,256]{2,1,0:T(8,128)(2,1)S(1)}, u32[]{:S(2)}) copy-start(bf16[3,128,256]{2,1,0:T(8,128)(2,1)S(1)} %fusion.16.pick_ref) | copy-start | bytes 589828
  17.9 14.3 %copy-start = (bf16[2,256,512]{2,1,0:T(8,128)(2,1)}, bf16[2,256,512]{2,1,0:T(8,128)(2,1)S(1)}, u32[]{:S(2)}) copy-start(bf16[2,256,512]{2,1,0:T(8,128)(2,1)S(1)} %fusion.9.expand_ref) | copy-start | bytes 1572868
  23.1 9.0 %copy-start.5 = (f32[64,128]{1,0:T(8,128)}, f32[64,128]{1,0:T(8,128)S(1)}, u32[]{:S(2)}) copy-start(f32[64,128]{1,0:T(8,128)S(1)} %broadcast_in_dim.78.rate_ref) | copy-start | bytes 98308
  32.2 11.2 %collective-permute-start.2 = (f32[8,64,384]{2,1,0:T(8,128)}, f32[8,64,384]{2,1,0:T(8,128)S(1)}, u32[]{:S(2)}, u32[]{:S(2)}) collective-permute-start(f32[8,64,384]{2,1,0:T(8,128)} %get-tuple-element.15.own_ref), channel_id=1, source_target_pairs={{0,1},{1,2},{2,3},{3,4},{4,5},{5,6},{6,7},{7,8},{8,9},{9,10},{10,1... | collective-permute-start | bytes 2359304 | tf_op jit(solution)/shard_map/ppermute | solution.py:28
  34.1 13.8 %collective-permute-start.3 = (f32[8,64,384]{2,1,0:T(8,128)}, f32[8,64,384]{2,1,0:T(8,128)S(1)}, u32[]{:S(2)}, u32[]{:S(2)}) collective-permute-start(f32[8,64,384]{2,1,0:T(8,128)} %get-tuple-element.15.own_ref), channel_id=1, source_target_pairs={{1,0},{2,1},{3,2},{4,3},{5,4},{6,5},{7,6},{8,7},{9,8},{10,9},{11,1... | collective-permute-start | bytes 2359304 | tf_op jit(solution)/shard_map/ppermute | solution.py:28
  55.9 31.8 %all-to-all-start = ((f32[128,1,384]{2,1,0:T(1,128)}), f32[128,1,384]{2,1,0:T(1,128)S(1)}, u32[]{:S(2)}, u32[]{:S(2)}) async-start(f32[128,1,384]{2,1,0:T(1,128)} %get-tuple-element.17), calls=%async_computation | async-start | bytes 393216 | tf_op jit(solution)/shard_map/all_to_all | solution.py:539
  77.7 9.9 %copy-start.7 = (f32[2,64,64]{2,1,0:T(8,128)S(1)}, f32[2,64,64]{2,1,0:T(8,128)}, u32[]{:S(2)}) copy-start(f32[2,64,64]{2,1,0:T(8,128)} %constant.296.clone.twiddle_ref) | copy-start | bytes 98308
  77.7 9.9 %copy-start.11 = (f32[32,128]{1,0:T(8,128)S(1)}, f32[32,128]{1,0:T(8,128)}, u32[]{:S(2)}) copy-start(f32[32,128]{1,0:T(8,128)} %constant.297.clone.forward_ref) | copy-start | bytes 49156
  77.7 10.0 %copy-start.12 = (f32[16,128]{1,0:T(8,128)S(1)}, f32[16,128]{1,0:T(8,128)}, u32[]{:S(2)}) copy-start(f32[16,128]{1,0:T(8,128)} %constant.295.clone.split_ref) | copy-start | bytes 24580
  89.6 17.2 %all-to-all-start.1 = ((f32[256,1,8]{2,1,0:T(1,128)}), f32[256,1,8]{2,1,0:T(1,128)S(1)}, u32[]{:S(2)}, u32[]{:S(2)}) async-start(f32[256,1,8]{2,1,0:T(1,128)} %bitcast.49), calls=%async_computation.1 | async-start | bytes 262144 | tf_op jit(solution)/shard_map/all_to_all | solution.py:545
  114.9 20.5 %copy-start.6 = (f32[2,64,64]{2,1,0:T(8,128)S(1)}, f32[2,64,64]{2,1,0:T(8,128)}, u32[]{:S(2)}) copy-start(f32[2,64,64]{2,1,0:T(8,128)} %constant.300.clone.untwist_ref) | copy-start | bytes 98308
  114.9 20.5 %copy-start.8 = (f32[64,64]{1,0:T(8,128)S(1)}, f32[64,64]{1,0:T(8,128)}, u32[]{:S(2)}) copy-start(f32[64,64]{1,0:T(8,128)} %constant.299.clone.backward_ref) | copy-start | bytes 49156
  114.9 20.5 %copy-start.9 = (f32[32,64]{1,0:T(8,128)S(1)}, f32[32,64]{1,0:T(8,128)}, u32[]{:S(2)}) copy-start(f32[32,64]{1,0:T(8,128)} %constant.298.clone.factor_ref) | copy-start | bytes 24580
  114.9 20.4 %copy-start.10 = (f32[32,128]{1,0:T(8,128)S(1)}, f32[32,128]{1,0:T(8,128)}, u32[]{:S(2)}) copy-start(f32[32,128]{1,0:T(8,128)} %constant.301.clone.join_ref) | copy-start | bytes 49156
  137.0 17.6 %all-to-all-start.3 = ((f32[128,1,256]{2,1,0:T(1,128)}), f32[128,1,256]{2,1,0:T(1,128)S(1)}, u32[]{:S(2)}, u32[]{:S(2)}) async-start(f32[128,1,256]{2,1,0:T(1,128)} %get-tuple-element.23), calls=%async_computation.3 | async-start | bytes 262144 | tf_op jit(solution)/shard_map/all_to_all | solution.py:554
  144.9 9.8 %copy-start.4 = (bf16[2,128,64]{2,1,0:T(8,128)(2,1)S(1)}, bf16[2,128,64]{2,1,0:T(8,128)(2,1)}, u32[]{:S(2)}) copy-start(bf16[2,128,64]{2,1,0:T(8,128)(2,1)} %fusion.19.place_ref) | copy-start | bytes 98308
  (5 other events, 14.6 us)

commit v5 on v4

--- a/solution.py
+++ b/solution.py
@@ -417,7 +417,7 @@
 
 
 def spectral_kernel(
-    first_ref, prev_ref, before_ref, gain_ref, re_ref, im_ref, diagonal_ref, cosine_ref, out_re, out_im
+    first_ref, prev_ref, before_ref, gain_ref, re_ref, im_ref, diagonal_ref, cosine_ref, out_ref
 ):
     even = iota((8, 128), 0) % 2 == 0
     order = first_ref[0] + iota((8, 128), 0) % 2
@@ -445,8 +445,10 @@
         return previous, before, acc_re, acc_im
 
     carried = lax.fori_loop(0, DEGREES // 16, some_degrees, (zero, zero, zero, zero))
-    out_re[...] = carried[2]
-    out_im[...] = carried[3]
+    acc_re, acc_im = carried[2], carried[3]
+    top = iota((8, 128), 0) < 4
+    out_ref[0] = jnp.where(top, acc_re, pltpu.roll(acc_im, 4, 0))
+    out_ref[1] = jnp.where(top, pltpu.roll(acc_re, 4, 0), acc_im)
 
 
 def solve_spectral(received, first_order, lat_total):
@@ -461,12 +463,11 @@
     coef_prev, coef_before = recurrence_factors(orders)
     degree_real = jnp.arange(DEGREES, dtype=jnp.int32).astype(jnp.float32)
     gain = POT_GAIN / (degree_real * (degree_real + 1.0) + KAPPA2)
-    shape = jax.ShapeDtypeStruct((8, 128), jnp.float32)
-    acc_re, acc_im = pl.pallas_call(
+    both = pl.pallas_call(
         spectral_kernel,
-        out_shape=(shape, shape),
+        out_shape=jax.ShapeDtypeStruct((2, 8, 128), jnp.float32),
         in_specs=[SMEM_SPEC] * 4 + [VMEM_SPEC] * 4,
-        out_specs=(VMEM_SPEC, VMEM_SPEC),
+        out_specs=VMEM_SPEC,
         interpret=INTERPRET,
     )(
         orders[0:1],
@@ -475,8 +476,7 @@
         gain,
         *on_chip(rows[0] * weights, rows[1] * weights, diagonal, cosine),
     )
-    both = jnp.stack([acc_re, acc_im]).reshape(2, 2, 4, 128)
-    return both.transpose(1, 3, 0, 2).reshape(256, 8)
+    return both.transpose(0, 2, 1).reshape(256, 8)
 
 
 def body(

time: 156 us -> 155 us (level)
  no operation moved by 1% of the time
where the time goes in v5:
time: 155 us
  starting transfers between devices  42.7 us (28%)
  waiting for transfers between devices  40.7 us (26%)
  Pallas kernels  30 us (19%)
  blocking collectives  20.4 us (13%)
  local copies, waits for them, and re-layouts  12.8 us (8%)
  other arithmetic  7 us (5%)
    all_to_all x1, blocking collectives, body(): lax.all_to_all(synth, axes, split_axis=0, concat_axis=0, tiled=True)  20.4 us
    all_to_all x1, starting transfers between devices, body(): got = lax.all_to_all(faces, 'grp', split_axis=0, concat_axis=0, tiled=True)  19.9 us
    pallas_call x2, Pallas kernels, advance(): pl.pallas_call(functools.partial(step_kernel, last=last), out_shape=(jax....  16.3 us
    ppermute x4, waiting for transfers between devices, passed_along(): lax.ppermute(value, axis, [(source, source + steps) for source in range(l...  15.8 us
    ppermute x4, starting transfers between devices, passed_along(): lax.ppermute(value, axis, [(source, source + steps) for source in range(l...  11.3 us
    all_to_all x1, waiting for transfers between devices, body(): got = lax.all_to_all(faces, 'grp', split_axis=0, concat_axis=0, tiled=True)  9.91 us
    all_to_all x1, waiting for transfers between devices, body(): home = lax.all_to_all(back, 'grp', split_axis=0, concat_axis=0, tiled=True)  9.8 us
    gather x1, local copies, waits for them, and re-layouts, legendre_start(): log_base = jnp.take(log_sums, orders)  6.87 us
  transfers between devices with their start and end apart: 7, of which 7 were waited for; matrix products, arithmetic and copies ran while one was open for 11% of the time, Pallas kernels for 0%

profile of v5, /device:TPU:1, one launch (start us, length us, event | category | flops | bytes accessed | tf_op | source)
XLA Modules:
  0.0 154.8 jit_solution(324324110748375984)
XLA Ops:
  1.5 3.0 %shard_map.165.own_ref = f32[8,64,384]{2,1,0:T(8,128)} custom-call(f32[8,64,512]{2,1,0:T(8,128)} %state_ref.3, bf16[512,256]{1,0:T(8,128)(2,1)} %fusion.15.select_ref), custom_call_target="tpu_custom_call" | custom-call | tf_op jit(solution)/shard_map/pallas_call | solution.py:230
  4.5 5.1 %collective-permute-start = (f32[8,64,384]{2,1,0:T(8,128)}, f32[8,64,384]{2,1,0:T(8,128)S(1)}, u32[]{:S(2)}, u32[]{:S(2)}) collective-permute-start(f32[8,64,384]{2,1,0:T(8,128)} %shard_map.165.own_ref), channel_id=1, source_target_pairs={{0,1},{1,2},{2,3},{3,4},{4,5},{5,6},{6,7},{7,8},{8,9},{9,10},{10,1... | collective-permute-start | bytes 2359304 | tf_op jit(solution)/shard_map/ppermute | solution.py:28
  9.6 1.9 %collective-permute-start.1 = (f32[8,64,384]{2,1,0:T(8,128)}, f32[8,64,384]{2,1,0:T(8,128)S(1)}, u32[]{:S(2)}, u32[]{:S(2)}) collective-permute-start(f32[8,64,384]{2,1,0:T(8,128)} %shard_map.165.own_ref), channel_id=1, source_target_pairs={{1,0},{2,1},{3,2},{4,3},{5,4},{6,5},{7,6},{8,7},{9,8},{10,9},{11,1... | collective-permute-start | bytes 2359304 | tf_op jit(solution)/shard_map/ppermute | solution.py:28
  17.8 1.0 collective-permute-done.prev_ref
  18.8 4.3 %collective-permute-done.1.next_ref = f32[8,64,384]{2,1,0:T(8,128)S(1)} collective-permute-done((f32[8,64,384]{2,1,0:T(8,128)}, f32[8,64,384]{2,1,0:T(8,128)S(1)}, u32[]{:S(2)}, u32[]{:S(2)}) %collective-permute-start.1) | collective-permute-done | bytes 786464 | tf_op jit(solution)/shard_map/ppermute | solution.py:28
  23.8 8.3 %shard_map.166 = (f32[8,64,512]{2,1,0:T(8,128)}, f32[8,64,384]{2,1,0:T(8,128)}) custom-call(f32[192]{0:T(256)} %mul.173.mix_ref, f32[3]{0:T(128)} %broadcast_multiply_fusion.1.speed_ref, f32[8]{0:T(128)} %flow_ref.3, f32[8,64,512]{2,1,0:T(8,128)} %state_ref.3, f32[8,64,384]{2,1,0:T(8,128)S(1)} %collective-permute-done.prev_ref, f32[8,64,384]{2,1,0:T(8,128)S(1)} %copy-done.1, ...), custom_call_target="tpu_custom_call" | custom-call | tf_op jit(solution)/shard_map/pallas_call | solution.py:246
  32.2 1.9 %collective-permute-start.2 = (f32[8,64,384]{2,1,0:T(8,128)}, f32[8,64,384]{2,1,0:T(8,128)S(1)}, u32[]{:S(2)}, u32[]{:S(2)}) collective-permute-start(f32[8,64,384]{2,1,0:T(8,128)} %get-tuple-element.13.own_ref), channel_id=1, source_target_pairs={{0,1},{1,2},{2,3},{3,4},{4,5},{5,6},{6,7},{7,8},{8,9},{9,10},{10,1... | collective-permute-start | bytes 2359304 | tf_op jit(solution)/shard_map/ppermute | solution.py:28
  34.1 2.5 %collective-permute-start.3 = (f32[8,64,384]{2,1,0:T(8,128)}, f32[8,64,384]{2,1,0:T(8,128)S(1)}, u32[]{:S(2)}, u32[]{:S(2)}) collective-permute-start(f32[8,64,384]{2,1,0:T(8,128)} %get-tuple-element.13.own_ref), channel_id=1, source_target_pairs={{1,0},{2,1},{3,2},{4,3},{5,4},{6,5},{7,6},{8,7},{9,8},{10,9},{11,1... | collective-permute-start | bytes 2359304 | tf_op jit(solution)/shard_map/ppermute | solution.py:28
  37.4 6.0 %collective-permute-done.2.prev_ref = f32[8,64,384]{2,1,0:T(8,128)S(1)} collective-permute-done((f32[8,64,384]{2,1,0:T(8,128)}, f32[8,64,384]{2,1,0:T(8,128)S(1)}, u32[]{:S(2)}, u32[]{:S(2)}) %collective-permute-start.2) | collective-permute-done | bytes 786464 | tf_op jit(solution)/shard_map/ppermute | solution.py:28
  43.3 4.6 %collective-permute-done.3.next_ref = f32[8,64,384]{2,1,0:T(8,128)S(1)} collective-permute-done((f32[8,64,384]{2,1,0:T(8,128)}, f32[8,64,384]{2,1,0:T(8,128)S(1)}, u32[]{:S(2)}, u32[]{:S(2)}) %collective-permute-start.3) | collective-permute-done | bytes 786464 | tf_op jit(solution)/shard_map/ppermute | solution.py:28
  47.9 8.0 %shard_map.167 = (f32[8,64,512]{2,1,0:T(8,128)}, f32[128,1,384]{2,1,0:T(1,128)}) custom-call(f32[192]{0:T(256)} %mul.173.mix_ref, f32[3]{0:T(128)} %broadcast_multiply_fusion.1.speed_ref, f32[8]{0:T(128)} %flow_ref.3, f32[8,64,512]{2,1,0:T(8,128)} %get-tuple-element.12.state_ref, f32[8,64,384]{2,1,0:T(8,128)S(1)} %collective-permute-done.2.prev_ref, ...), custom_call_target="tpu_custom_call" | custom-call | tf_op jit(solution)/shard_map/pallas_call | solution.py:246
  55.9 19.9 %all-to-all-start = ((f32[128,1,384]{2,1,0:T(1,128)}), f32[128,1,384]{2,1,0:T(1,128)S(1)}, u32[]{:S(2)}, u32[]{:S(2)}) async-start(f32[128,1,384]{2,1,0:T(1,128)} %get-tuple-element.15), calls=%async_computation | async-start | bytes 393216 | tf_op jit(solution)/shard_map/all_to_all | solution.py:539
  77.7 9.9 %all-to-all-done = f32[128,1,384]{2,1,0:T(1,128)S(1)} async-done(((f32[128,1,384]{2,1,0:T(1,128)}), f32[128,1,384]{2,1,0:T(1,128)S(1)}, u32[]{:S(2)}, u32[]{:S(2)}) %all-to-all-start) | async-done | bytes 196640 | tf_op jit(solution)/shard_map/all_to_all | solution.py:539
  87.7 1.9 %shard_map.168 = (f32[16,128]{1,0:T(8,128)}, f32[256,8]{1,0:T(8,128)}) custom-call(f32[128,384]{1,0:T(8,128)S(1)} %bitcast.39, f32[16,128]{1,0:T(8,128)S(1)} %copy-done.12, f32[2,64,64]{2,1,0:T(8,128)S(1)} %copy-done.7, f32[32,128]{1,0:T(8,128)S(1)} %copy-done.11), custom_call_target="tpu_custom_call" | custom-call | tf_op jit(solution)/shard_map/pallas_call | solution.py:375
  89.6 5.2 %all-to-all-start.1 = ((f32[256,1,8]{2,1,0:T(1,128)}), f32[256,1,8]{2,1,0:T(1,128)S(1)}, u32[]{:S(2)}, u32[]{:S(2)}) async-start(f32[256,1,8]{2,1,0:T(1,128)} %bitcast.43), calls=%async_computation.1 | async-start | bytes 262144 | tf_op jit(solution)/shard_map/all_to_all | solution.py:545
  94.8 6.9 %gather_fusion = f32[1024]{0:T(1024)S(1)} fusion(f32[512]{0:T(512)S(1)} %pad_maximum_fusion, s32[1024]{0:T(1024)S(1)} %bitcast_clamp_fusion), kind=kCustom, calls=%fused_computation | custom fusion | bytes 12288 | tf_op jit(solution)/shard_map/jit(_take)/gather | solution.py:393
  101.6 5.2 %all-to-all-done.1 = f32[256,1,8]{2,1,0:T(1,128)S(1)} async-done(((f32[256,1,8]{2,1,0:T(1,128)}), f32[256,1,8]{2,1,0:T(1,128)S(1)}, u32[]{:S(2)}, u32[]{:S(2)}) %all-to-all-start.1) | async-done | bytes 8224 | tf_op jit(solution)/shard_map/all_to_all | solution.py:545
  107.0 6.3 %shard_map.169 = f32[2,8,128]{2,1,0:T(8,128)} custom-call(s32[1]{0:T(128)} %bitcast.51, f32[1024]{0:T(1024)} %get-tuple-element.27.prev_ref, f32[1024]{0:T(1024)} %get-tuple-element.26.before_ref, f32[512]{0:T(512)} %fusion.35.gain_ref, f32[8,128]{1,0:T(8,128)S(1)} %get-tuple-element.30.re_ref, f32[8,128]{1,0:T(8,128)S(1)} %get-tuple-element.29.im_ref, ...), custom_call_target="tpu_custom_call" | custom-call | tf_op jit(solution)/shard_map/pallas_call | solution.py:466
  113.3 0.8 copy.49
  114.2 20.4 %all_to_all.30 = f32[256,1,8]{2,1,0:T(1,128)S(1)} all-to-all(f32[256,1,8]{2,1,0:T(1,128)S(1)} %copy.49), channel_id=1, replica_groups=mesh['grp'=128,'cores'=2] {'grp','cores'}, dimensions={0} | all-to-all | bytes 16384 | tf_op jit(solution)/shard_map/all_to_all | solution.py:547
  134.7 1.6 %shard_map.170 = (f32[16,128]{1,0:T(8,128)}, f32[128,1,256]{2,1,0:T(1,128)}) custom-call(f32[256,8]{1,0:T(8,128)S(1)} %bitcast.41, f32[128,384]{1,0:T(8,128)S(1)} %bitcast.40, f32[32,64]{1,0:T(8,128)S(1)} %copy-done.9, f32[64,64]{1,0:T(8,128)S(1)} %copy-done.8, f32[2,64,64]{2,1,0:T(8,128)S(1)} %copy-done.6, f32[32,128]{1,0:T(8,128)S(1)} %copy-done.10), custom_call_target="tpu_custom_call" | custom-call | tf_op jit(solution)/shard_map/pallas_call | solution.py:375
  136.3 6.3 %all-to-all-start.3 = ((f32[128,1,256]{2,1,0:T(1,128)}), f32[128,1,256]{2,1,0:T(1,128)S(1)}, u32[]{:S(2)}, u32[]{:S(2)}) async-start(f32[128,1,256]{2,1,0:T(1,128)} %get-tuple-element.19), calls=%async_computation.3 | async-start | bytes 262144 | tf_op jit(solution)/shard_map/all_to_all | solution.py:554
  144.1 9.8 %all-to-all-done.3 = f32[128,1,256]{2,1,0:T(1,128)S(1)} async-done(((f32[128,1,256]{2,1,0:T(1,128)}), f32[128,1,256]{2,1,0:T(1,128)S(1)}, u32[]{:S(2)}, u32[]{:S(2)}) %all-to-all-start.3) | async-done | bytes 131104 | tf_op jit(solution)/shard_map/all_to_all | solution.py:554
  154.0 0.8 shard_map.171
  (114 shorter events, 12.1 us)
Async XLA Ops:
  1.4 11.4 %copy-start.16 = (s32[64,6]{0,1:T(8,128)S(1)}, s32[64,6]{0,1:T(8,128)}, u32[]{:S(2)}) copy-start(s32[64,6]{0,1:T(8,128)} %param.17) | copy-start | bytes 4612
  1.4 11.5 %copy-start.18 = (s32[64,1]{0,1:T(1,128)S(1)}, s32[64,1]{0,1:T(1,128)}, u32[]{:S(2)}) copy-start(s32[64,1]{0,1:T(1,128)} %param.18) | copy-start | bytes 772
  1.4 12.3 %copy-start.13 = (f32[3,8,8]{2,1,0:T(8,128)S(1)}, f32[3,8,8]{2,1,0:T(8,128)}, u32[]{:S(2)}) copy-start(f32[3,8,8]{2,1,0:T(8,128)} %param.15) | copy-start | bytes 2308
  1.4 14.3 %copy-start.19 = (s32[64]{0:T(128)S(1)}, s32[64]{0:T(128)}, u32[]{:S(2)}) copy-start(s32[64]{0:T(128)} %param.19) | copy-start | bytes 772
  1.4 14.9 %copy-start.20 = (s32[64]{0:T(128)S(1)}, s32[64]{0:T(128)}, u32[]{:S(2)}) copy-start(s32[64]{0:T(128)} %param.16) | copy-start | bytes 772
  4.5 19.3 %copy-start.1 = (f32[8,64,384]{2,1,0:T(8,128)S(1)}, f32[8,64,384]{2,1,0:T(8,128)}, u32[]{:S(2)}) copy-start(f32[8,64,384]{2,1,0:T(8,128)} %shard_map.165.own_ref) | copy-start | bytes 2359300
  4.5 14.3 %collective-permute-start = (f32[8,64,384]{2,1,0:T(8,128)}, f32[8,64,384]{2,1,0:T(8,128)S(1)}, u32[]{:S(2)}, u32[]{:S(2)}) collective-permute-start(f32[8,64,384]{2,1,0:T(8,128)} %shard_map.165.own_ref), channel_id=1, source_target_pairs={{0,1},{1,2},{2,3},{3,4},{4,5},{5,6},{6,7},{7,8},{8,9},{9,10},{10,1... | collective-permute-start | bytes 2359304 | tf_op jit(solution)/shard_map/ppermute | solution.py:28
  9.6 13.5 %collective-permute-start.1 = (f32[8,64,384]{2,1,0:T(8,128)}, f32[8,64,384]{2,1,0:T(8,128)S(1)}, u32[]{:S(2)}, u32[]{:S(2)}) collective-permute-start(f32[8,64,384]{2,1,0:T(8,128)} %shard_map.165.own_ref), channel_id=1, source_target_pairs={{1,0},{2,1},{3,2},{4,3},{5,4},{6,5},{7,6},{8,7},{9,8},{10,9},{11,1... | collective-permute-start | bytes 2359304 | tf_op jit(solution)/shard_map/ppermute | solution.py:28
  17.3 6.5 %copy-start.3 = (bf16[3,128,256]{2,1,0:T(8,128)(2,1)}, bf16[3,128,256]{2,1,0:T(8,128)(2,1)S(1)}, u32[]{:S(2)}) copy-start(bf16[3,128,256]{2,1,0:T(8,128)(2,1)S(1)} %fusion.16.pick_ref) | copy-start | bytes 589828
  17.8 14.4 %copy-start = (bf16[2,256,512]{2,1,0:T(8,128)(2,1)}, bf16[2,256,512]{2,1,0:T(8,128)(2,1)S(1)}, u32[]{:S(2)}) copy-start(bf16[2,256,512]{2,1,0:T(8,128)(2,1)S(1)} %fusion.9.expand_ref) | copy-start | bytes 1572868
  23.1 9.0 %copy-start.5 = (f32[64,128]{1,0:T(8,128)}, f32[64,128]{1,0:T(8,128)S(1)}, u32[]{:S(2)}) copy-start(f32[64,128]{1,0:T(8,128)S(1)} %broadcast_in_dim.78.rate_ref) | copy-start | bytes 98308
  32.2 11.2 %collective-permute-start.2 = (f32[8,64,384]{2,1,0:T(8,128)}, f32[8,64,384]{2,1,0:T(8,128)S(1)}, u32[]{:S(2)}, u32[]{:S(2)}) collective-permute-start(f32[8,64,384]{2,1,0:T(8,128)} %get-tuple-element.13.own_ref), channel_id=1, source_target_pairs={{0,1},{1,2},{2,3},{3,4},{4,5},{5,6},{6,7},{7,8},{8,9},{9,10},{10,1... | collective-permute-start | bytes 2359304 | tf_op jit(solution)/shard_map/ppermute | solution.py:28
  34.1 13.8 %collective-permute-start.3 = (f32[8,64,384]{2,1,0:T(8,128)}, f32[8,64,384]{2,1,0:T(8,128)S(1)}, u32[]{:S(2)}, u32[]{:S(2)}) collective-permute-start(f32[8,64,384]{2,1,0:T(8,128)} %get-tuple-element.13.own_ref), channel_id=1, source_target_pairs={{1,0},{2,1},{3,2},{4,3},{5,4},{6,5},{7,6},{8,7},{9,8},{10,9},{11,1... | collective-permute-start | bytes 2359304 | tf_op jit(solution)/shard_map/ppermute | solution.py:28
  55.9 31.8 %all-to-all-start = ((f32[128,1,384]{2,1,0:T(1,128)}), f32[128,1,384]{2,1,0:T(1,128)S(1)}, u32[]{:S(2)}, u32[]{:S(2)}) async-start(f32[128,1,384]{2,1,0:T(1,128)} %get-tuple-element.15), calls=%async_computation | async-start | bytes 393216 | tf_op jit(solution)/shard_map/all_to_all | solution.py:539
  77.7 9.9 %copy-start.7 = (f32[2,64,64]{2,1,0:T(8,128)S(1)}, f32[2,64,64]{2,1,0:T(8,128)}, u32[]{:S(2)}) copy-start(f32[2,64,64]{2,1,0:T(8,128)} %constant.296.clone.twiddle_ref) | copy-start | bytes 98308
  77.7 9.9 %copy-start.11 = (f32[32,128]{1,0:T(8,128)S(1)}, f32[32,128]{1,0:T(8,128)}, u32[]{:S(2)}) copy-start(f32[32,128]{1,0:T(8,128)} %constant.297.clone.forward_ref) | copy-start | bytes 49156
  77.7 10.0 %copy-start.12 = (f32[16,128]{1,0:T(8,128)S(1)}, f32[16,128]{1,0:T(8,128)}, u32[]{:S(2)}) copy-start(f32[16,128]{1,0:T(8,128)} %constant.295.clone.split_ref) | copy-start | bytes 24580
  89.6 17.2 %all-to-all-start.1 = ((f32[256,1,8]{2,1,0:T(1,128)}), f32[256,1,8]{2,1,0:T(1,128)S(1)}, u32[]{:S(2)}, u32[]{:S(2)}) async-start(f32[256,1,8]{2,1,0:T(1,128)} %bitcast.43), calls=%async_computation.1 | async-start | bytes 262144 | tf_op jit(solution)/shard_map/all_to_all | solution.py:545
  114.2 20.5 %copy-start.6 = (f32[2,64,64]{2,1,0:T(8,128)S(1)}, f32[2,64,64]{2,1,0:T(8,128)}, u32[]{:S(2)}) copy-start(f32[2,64,64]{2,1,0:T(8,128)} %constant.300.clone.untwist_ref) | copy-start | bytes 98308
  114.2 20.5 %copy-start.8 = (f32[64,64]{1,0:T(8,128)S(1)}, f32[64,64]{1,0:T(8,128)}, u32[]{:S(2)}) copy-start(f32[64,64]{1,0:T(8,128)} %constant.299.clone.backward_ref) | copy-start | bytes 49156
  114.2 20.5 %copy-start.9 = (f32[32,64]{1,0:T(8,128)S(1)}, f32[32,64]{1,0:T(8,128)}, u32[]{:S(2)}) copy-start(f32[32,64]{1,0:T(8,128)} %constant.298.clone.factor_ref) | copy-start | bytes 24580
  114.2 20.5 %copy-start.10 = (f32[32,128]{1,0:T(8,128)S(1)}, f32[32,128]{1,0:T(8,128)}, u32[]{:S(2)}) copy-start(f32[32,128]{1,0:T(8,128)} %constant.301.clone.join_ref) | copy-start | bytes 49156
  136.3 17.7 %all-to-all-start.3 = ((f32[128,1,256]{2,1,0:T(1,128)}), f32[128,1,256]{2,1,0:T(1,128)S(1)}, u32[]{:S(2)}, u32[]{:S(2)}) async-start(f32[128,1,256]{2,1,0:T(1,128)} %get-tuple-element.19), calls=%async_computation.3 | async-start | bytes 262144 | tf_op jit(solution)/shard_map/all_to_all | solution.py:554
  144.1 9.8 %copy-start.4 = (bf16[2,128,64]{2,1,0:T(8,128)(2,1)S(1)}, bf16[2,128,64]{2,1,0:T(8,128)(2,1)}, u32[]{:S(2)}) copy-start(bf16[2,128,64]{2,1,0:T(8,128)(2,1)} %fusion.19.place_ref) | copy-start | bytes 98308
  (4 other events, 14.0 us)
